TPU v7x, 32 devices: a whole 2x2x4 slice. The times are simulated.
32 devices in a mesh: groups: 2 (over y), segment: 8 (over z, x), space: 2 (over core).
Axes of the slice: x: 2, y: 2, z: 4, core: 2. Of those that a mesh axis runs over, the one named last changes fastest.
Arguments:
- patches: bfloat16 [16, 256, 1536], P(('groups', 'segment'), 'space'), parts along dimension 0, may hold values from -120 to 120
- positions: int32 [16], P(('groups', 'segment')), parts along dimension 0, may hold values from 0 to 1
- timesteps: int32 [16], P(('groups', 'segment')), parts along dimension 0, may hold values from 0 to 1
- section_bounds: int32 [9], replicated, may hold values from 0 to 12, as said below
- tile_neighbours: int32 [4, 2], replicated, may hold values from 0 to 3, as said below
- modulation: bfloat16 [6, 12, 3, 1536], P('groups'), parts along dimension 0, may hold values from -9 to 9
- query_gain: float32 [12, 128], replicated, may hold values from 0.5 to 2
- stale_kv: bfloat16 [16, 2, 2, 512, 1536], P(('groups', 'segment'), None, None, 'space'), parts along dimension 0, may hold values from -70 to 70
Outputs:
- advanced: bfloat16 [16, 256, 1536], P(('groups', 'segment'), 'space'), parts along dimension 0
There are 2 independent parts, one for each index of `groups`. A program takes and returns all parts, laid end to end along the dimension named above; an argument that names none is the same for every part. Nothing has to cross between parts.
Inputs may be any that keep to these rules, and one draw needn't show every extreme that they name: section_bounds[0] is 0 and section_bounds[8] is 12; section j holds layers section_bounds[j] to section_bounds[j+1] - 1, one or 2 of them, and some sections hold 2. `tile_neighbours`: tile g lies in time layer g // 2; row g names first a tile of its own time layer, then a tile of the other time layer.
All inputs are finite; a program needn't handle non-finite values.
Results may differ from a plain program's by a relative error of at most 0.0051.
Values may be sent and summed in bfloat16 or wider, within the bound.
No kernel may reach another device: no remote copies, remote signals or barrier semaphores. Data moves between devices by JAX's collectives and lax.ppermute only.
A program may use at most 64 MiB of HBM per device.

v0:
```python
import jax
import jax.numpy as jnp
from jax import lax
from jax.sharding import PartitionSpec as P

HEADS = 12
HDIM = 128
D = 1536
TILE = 128
SLAB_DEV = 2
NB = 2
PIPE = 8
LMAX = 2
LAYERS = 12
STEPS = 3
TICKS = 2


epsilon = 1e-06


def extended_2(x, sides, width):
    for axis, dim in sides:
        devices, length = (lax.axis_size(axis), x.shape[dim])
        up = [(i, (i + 1) % devices) for i in range(devices - 1)]
        down = [(j, i) for i, j in up]
        last = lax.slice_in_dim(x, length - width, length, axis=dim)
        initial = lax.slice_in_dim(x, 0, width, axis=dim)
        before = lax.ppermute(last, axis, up)
        after = lax.ppermute(initial, axis, down)
        x = jnp.concatenate([before, x, after], axis=dim)
    return x


def from_behind(x, axis, by):
    devices = lax.axis_size(axis)
    return lax.ppermute(x, axis, [(i, (i + by) % devices) for i in range(devices)])


def attend(stream, key_tiles, value_tiles, tile_choice, mod_rows, gain_row):
    batch_size = stream.shape[0]
    middle = jnp.mean(stream, axis=-1, keepdims=True)
    centred = stream - middle
    spread = jnp.mean(centred * centred, axis=-1, keepdims=True)
    normed = centred * lax.rsqrt(spread + epsilon)
    shifted = normed * (1.0 + mod_rows[:, 1:2, :]) + mod_rows[:, 0:1, :]
    heads_in = shifted.reshape(batch_size, TILE, HEADS, HDIM)
    head_rms = jnp.mean(heads_in * heads_in, axis=-1, keepdims=True)
    queries = (heads_in * lax.rsqrt(head_rms + epsilon) * gain_row).astype(jnp.bfloat16)
    key_rows = key_tiles[tile_choice].reshape(batch_size, NB * TILE, HEADS, HDIM)
    value_rows = value_tiles[tile_choice].reshape(batch_size, NB * TILE, HEADS, HDIM)
    scores = jnp.einsum(
        "bqhd,bkhd->bhqk", queries, key_rows, preferred_element_type=jnp.float32
    ) * HDIM ** (-0.5)
    row_max = jnp.max(scores, axis=-1, keepdims=True)
    powers = jnp.exp(scores - row_max)
    totals = jnp.sum(powers, axis=-1)
    weights = powers.astype(jnp.bfloat16)
    blended = jnp.einsum("bhqk,bkhd->bqhd", weights, value_rows, preferred_element_type=jnp.float32)
    blended = blended / jnp.transpose(totals, (0, 2, 1))[..., None]
    return stream + mod_rows[:, 2:3, :] * blended.reshape(batch_size, TILE, D)


def run_slots(holding, ext_index, step_onehot, extended, slot_mods, slot_gains, layer_count):
    stream = holding.astype(jnp.float32)
    for slot_index in range(LMAX):
        mod_rows = jnp.einsum("bs,sjd->bjd", step_onehot, slot_mods[slot_index].astype(jnp.float32))
        updated = attend(
            stream,
            extended[slot_index, 0],
            extended[slot_index, 1],
            ext_index,
            mod_rows,
            slot_gains[slot_index],
        )
        stream = jnp.where(slot_index < layer_count, updated, stream)
    return stream.astype(jnp.bfloat16)


def per_device(
    patches, positions, timesteps, section_bounds, tile_neighbours, modulation, query_gain, stale_kv
):
    tile_len = patches.shape[1]
    feature_width = patches.shape[2]
    local_kv = stale_kv[0]
    framed = extended_2(local_kv[:, :, None], (("space", 2),), 1)
    extended = framed.reshape(LMAX, 2, 3 * SLAB_DEV, tile_len, feature_width)
    device = lax.axis_index("segment")
    space_index = lax.axis_index("space")
    cycle_size = lax.axis_size("segment")
    section = device % PIPE
    first_layer = section_bounds[section]
    layer_count = section_bounds[section + 1] - first_layer
    slot_mods = []
    slot_gains = []
    for slot_index in range(LMAX):
        layer_now = jnp.minimum(first_layer + slot_index, LAYERS - 1)
        slot_mods.append(lax.dynamic_index_in_dim(modulation, layer_now, 1, False))
        slot_gains.append(lax.dynamic_index_in_dim(query_gain, layer_now, 0, False))
    step_range = jnp.arange(STEPS, dtype=jnp.int32)
    holding = patches
    held_pos = positions
    held_steps = timesteps
    for tick_index in range(TICKS):
        if tick_index > 0:
            held_pos, held_steps = from_behind((held_pos, held_steps), "segment", 1)
        root = (device - tick_index) % cycle_size
        step_rows = held_steps + (root % PIPE + tick_index >= PIPE).astype(jnp.int32)
        listed_tiles = tile_neighbours[space_index * SLAB_DEV + held_pos]
        ext_index = (
            listed_tiles // SLAB_DEV - space_index + 1
        ) * SLAB_DEV + listed_tiles % SLAB_DEV
        step_onehot = (step_rows[:, None] == step_range[None, :]).astype(jnp.float32)
        finished = run_slots(
            holding, ext_index, step_onehot, extended, slot_mods, slot_gains, layer_count
        )
        holding = from_behind(finished, "segment", 1)
    return holding


def solution(mesh):
    placed = (
        P(("groups", "segment"), "space", None),
        P(("groups", "segment")),
        P(("groups", "segment")),
        P(),
        P(),
        P("groups", None, None, None),
        P(),
        P(("groups", "segment"), None, None, "space", None),
    )
    return jax.shard_map(
        per_device,
        mesh=mesh,
        in_specs=placed,
        out_specs=P(("groups", "segment"), "space", None),
        check_vma=False,
    )
```

profile of v0, /device:TPU:0, one launch (start us, length us, event | category | flops | bytes accessed | tf_op | source)
XLA Modules:
  0.0 122.3 jit_solution(10010308473332576144)
XLA Ops:
  1.3 6.3 %collective-permute-start = (bf16[2,2,1,256,1536]{4,3,2,1,0:T(8,128)(2,1)}, bf16[2,2,1,256,1536]{4,3,2,1,0:T(8,128)(2,1)}, u32[]{:S(2)}, u32[]{:S(2)}) collective-permute-start(bf16[2,2,1,256,1536]{4,3,2,1,0:T(8,128)(2,1)} %bitcast.237), channel_id=1, source_target_pairs={{0,1},{2,3},{4,5},{6,7},{8,9},{10,11},{12,13},{14,15},{16,17},{18,... | collective-permute-start | bytes 9437192 | tf_op jit(solution)/shard_map/ppermute | solution.py:29
  7.6 3.0 %collective-permute-start.4 = (s32[1]{0:T(128)}, s32[1]{0:T(128)}, u32[]{:S(2)}, u32[]{:S(2)}) collective-permute-start(s32[1]{0:T(128)} %param.9), channel_id=1, source_target_pairs={{0,2},{2,4},{4,6},{6,8},{8,10},{10,12},{12,14},{14,0},{1,3},{3,5},... | collective-permute-start | bytes 20 | tf_op jit(solution)/shard_map/ppermute | solution.py:37
  10.6 1.5 %collective-permute-start.3 = (s32[1]{0:T(128)}, s32[1]{0:T(128)}, u32[]{:S(2)}, u32[]{:S(2)}) collective-permute-start(s32[1]{0:T(128)} %param.10), channel_id=1, source_target_pairs={{0,2},{2,4},{4,6},{6,8},{8,10},{10,12},{12,14},{14,0},{1,3},{3,5},... | collective-permute-start | bytes 20 | tf_op jit(solution)/shard_map/ppermute | solution.py:37
  12.8 1.4 %fusion.86 = (s32[1]{0:T(128)}, s32[1]{0:T(128)}) fusion(s32[9]{0:T(128)} %param.11, s32[]{:T(128)S(6)} %select_n.150, s32[]{:T(128)S(6)} %select_n.151), kind=kLoop, calls=%fused_computation.177 | loop fusion | bytes 24 | tf_op jit(solution)/shard_map/dynamic_slice | solution.py:93
  21.1 1.7 %fusion.80 = (f32[1,128,1536]{1,2,0:T(8,128)}, f32[1,128,1536]{1,2,0:T(8,128)}) fusion(f32[1536]{0:T(1024)S(1)} %get-tuple-element.69, f32[1536]{0:T(1024)S(1)} %get-tuple-element.70, f32[128]{0:T(128)S(1)} %add_rsqrt_fusion.7, f32[128]{0:T(128)S(1)} %broadcast_multiply_fusion.3, bf16[1,128,1536]{1,2,0:T(8,128)(2,1)S(1)} %copy.35), kind=kLoop, calls=%fused_computation.171 | loop fusion | flops 1179648 | bytes 1979392 | tf_op jit(solution)/shard_map/mul | solution.py:48
  22.8 1.8 %reduce_sum.154 = f32[128,12]{0,1:T(8,128)} reduce(f32[128,12,128]{0,2,1:T(8,128)} %bitcast.241, f32[]{:T(128)} %constant.129.clone.1), dimensions={2}, to_apply=%region_2.3 | reduce | flops 195072 | bytes 792580 | tf_op jit(solution)/shard_map/reduce_sum | solution.py:48
  30.0 1.5 %fusion.44 = f32[1,3,1536]{2,0,1:T(1,128)} fusion(bf16[3,3,1536]{2,1,0:T(4,128)(2,1)} %copy-done.8, s32[]{:T(128)} %bitcast.41), kind=kOutput, calls=%fused_computation.89 | convolution fusion | flops 27651 | bytes 46084 | tf_op jit(solution)/shard_map/bs,sjd->bjd/dot_general | solution.py:67
  31.5 7.0 %pad_maximum_fusion = bf16[2,2,3,256,1536]{4,3,2,1,0:T(8,128)(2,1)} fusion(bf16[2,2,1,256,1536]{4,3,2,1,0:T(8,128)(2,1)} %collective-permute-done.1, bf16[2,2,1,256,1536]{4,3,2,1,0:T(8,128)(2,1)S(1)} %bitcast.238, bf16[2,2,1,256,1536]{4,3,2,1,0:T(8,128)(2,1)} %collective-permute-done), kind=kLoop, calls=%fused_computation.8 | loop fusion | flops 9437184 | bytes 18874368 | tf_op jit(solution)/shard_map/concatenate | solution.py:31
  38.5 6.5 %slice_bitcast_fusion.2 = (bf16[6,128,1536]{2,1,0:T(8,128)(2,1)S(1)}, bf16[6,128,1536]{2,1,0:T(8,128)(2,1)}, bf16[6,128,1536]{2,1,0:T(8,128)(2,1)}, bf16[6,128,1536]{2,1,0:T(8,128)(2,1)}) fusion(bf16[2,2,6,128,1536]{4,3,2,1,0:T(8,128)(2,1)} %bitcast.235), kind=kLoop, calls=%fused_computation.11 | loop fusion | bytes 18874368 | tf_op jit(solution)/shard_map/squeeze | solution.py:70
  45.0 3.3 %gather_fusion.2 = bf16[2,128,1536]{2,1,0:T(8,128)(2,1)} fusion(bf16[6,128,1536]{2,1,0:T(8,128)(2,1)} %get-tuple-element.47, s32[1024]{0:T(1024)} %pad_clamp_fusion.1), kind=kCustom, calls=%fused_computation.2 | custom fusion | bytes 1572872 | tf_op jit(solution)/shard_map/gather | solution.py:51
  48.2 2.2 %copy.40 = bf16[2,128,1536]{1,0,2:T(2,128)(2,1)S(1)} copy(bf16[2,128,1536]{2,1,0:T(8,128)(2,1)} %gather_fusion.2) | data formatting | bytes 1572864 | tf_op jit(solution)/shard_map/gather | solution.py:51
  50.5 1.4 %reshape.917 = bf16[256,12,128]{0,2,1:T(8,128)(2,1)} reshape(bf16[2,128,1536]{1,0,2:T(2,128)(2,1)S(1)} %copy.40) | data formatting | bytes 1572864 | tf_op jit(solution)/shard_map/reshape.50
  51.9 2.4 %gather_fusion.3 = bf16[2,128,1536]{2,1,0:T(8,128)(2,1)S(1)} fusion(bf16[6,128,1536]{2,1,0:T(8,128)(2,1)} %get-tuple-element.46, s32[1024]{0:T(1024)} %pad_clamp_fusion.1), kind=kCustom, calls=%fused_computation.3 | custom fusion | bytes 1572872 | tf_op jit(solution)/shard_map/gather | solution.py:50
  54.3 1.5 %reshape.1052 = bf16[256,12,128]{2,1,0:T(8,128)(2,1)} reshape(bf16[2,128,1536]{2,1,0:T(8,128)(2,1)S(1)} %gather_fusion.3) | data formatting | bytes 1572864 | tf_op jit(solution)/shard_map/reshape.47
  55.8 3.3 %gather_fusion = bf16[2,128,1536]{2,1,0:T(8,128)(2,1)} fusion(bf16[6,128,1536]{2,1,0:T(8,128)(2,1)} %get-tuple-element.48, s32[1024]{0:T(1024)} %pad_clamp_fusion.1), kind=kCustom, calls=%fused_computation | custom fusion | bytes 1572872 | tf_op jit(solution)/shard_map/gather | solution.py:51
  59.1 2.2 %copy.36 = bf16[2,128,1536]{1,0,2:T(2,128)(2,1)S(1)} copy(bf16[2,128,1536]{2,1,0:T(8,128)(2,1)} %gather_fusion) | data formatting | bytes 1572864 | tf_op jit(solution)/shard_map/gather | solution.py:51
  63.5 1.6 %reshape.1051 = bf16[256,12,128]{2,1,0:T(8,128)(2,1)} reshape(bf16[2,128,1536]{2,1,0:T(8,128)(2,1)S(1)} %gather_fusion.1) | data formatting | bytes 1572864 | tf_op jit(solution)/shard_map/reshape.12
  65.1 2.0 %fusion.87 = (f32[12,128]{1,0:T(8,128)S(1)}, f32[12,128,256]{2,1,0:T(8,128)S(1)}) fusion(bf16[256,12,128]{2,1,0:T(8,128)(2,1)} %reshape.1051, f32[128,12,128]{0,2,1:T(8,128)} %bitcast.239, f32[128]{0:T(128)} %get-tuple-element.56, f32[128,12]{0,1:T(8,128)S(1)} %add_rsqrt_fusion.3), kind=kOutput, calls=%fused_computation.178 | convolution fusion | flops 102038016 | bytes 3158528 | tf_op jit(solution)/shard_map/bqhd,bkhd->bhqk/dot_general | solution.py:52
  69.4 2.0 %fusion.85 = (f32[1,128,1536]{1,2,0:T(8,128)}, f32[1,128,1536]{1,2,0:T(8,128)}) fusion(f32[1536]{0:T(1024)S(1)} %copy-done.11, f32[1536]{0:T(1024)S(1)} %copy-done.10, f32[128]{0:T(128)S(1)} %add_rsqrt_fusion.6, f32[128]{0:T(128)S(1)} %broadcast_multiply_fusion.2, f32[1,128,12,128]{1,3,2,0:T(8,128)S(1)} %fusion.8, f32[1536]{0:T(1024)S(1)} %get-tuple-element.71, ...), kind=kLoop, calls=%fused_computation.176 | loop fusion | flops 1769472 | bytes 2771969 | tf_op jit(solution)/shard_map/mul | solution.py:48
  72.6 2.0 %fusion.88 = (f32[12,128]{1,0:T(8,128)S(1)}, f32[12,128,256]{2,1,0:T(8,128)S(1)}) fusion(bf16[256,12,128]{2,1,0:T(8,128)(2,1)} %reshape.1052, f32[128,12,128]{0,2,1:T(8,128)} %bitcast.244, f32[128]{0:T(128)} %get-tuple-element.55, f32[128,12]{0,1:T(8,128)S(1)} %add_rsqrt_fusion.2), kind=kOutput, calls=%fused_computation.179 | convolution fusion | flops 102038016 | bytes 3158528 | tf_op jit(solution)/shard_map/bqhd,bkhd->bhqk/dot_general | solution.py:52
  77.7 1.5 %collective-permute-start.2 = (bf16[1,128,1536]{1,2,0:T(8,128)(2,1)}, bf16[1,128,1536]{1,2,0:T(8,128)(2,1)S(1)}, u32[]{:S(2)}, u32[]{:S(2)}) collective-permute-start(bf16[1,128,1536]{1,2,0:T(8,128)(2,1)} %fusion.22), channel_id=1, source_target_pairs={{0,2},{2,4},{4,6},{6,8},{8,10},{10,12},{12,14},{14,0},{1,3},{3,5},... | collective-permute-start | bytes 1179656 | tf_op jit(solution)/shard_map/ppermute | solution.py:37
  80.1 3.1 %gather_fusion.6 = bf16[2,128,1536]{2,1,0:T(8,128)(2,1)} fusion(bf16[6,128,1536]{2,1,0:T(8,128)(2,1)} %get-tuple-element.47, s32[1024]{0:T(1024)S(1)} %pad_clamp_fusion), kind=kCustom, calls=%fused_computation.6 | custom fusion | bytes 1572872 | tf_op jit(solution)/shard_map/gather | solution.py:51
  83.2 2.4 %gather_fusion.7 = bf16[2,128,1536]{2,1,0:T(8,128)(2,1)S(1)} fusion(bf16[6,128,1536]{2,1,0:T(8,128)(2,1)} %get-tuple-element.46, s32[1024]{0:T(1024)} %copy-done.17), kind=kCustom, calls=%fused_computation.7 | custom fusion | bytes 1572872 | tf_op jit(solution)/shard_map/gather | solution.py:50
  85.6 3.3 %gather_fusion.4 = bf16[2,128,1536]{2,1,0:T(8,128)(2,1)} fusion(bf16[6,128,1536]{2,1,0:T(8,128)(2,1)} %get-tuple-element.48, s32[1024]{0:T(1024)} %copy-done.17), kind=kCustom, calls=%fused_computation.4 | custom fusion | bytes 1572872 | tf_op jit(solution)/shard_map/gather | solution.py:51
  88.9 1.6 %gather_fusion.5 = bf16[2,128,1536]{2,1,0:T(8,128)(2,1)} fusion(bf16[6,128,1536]{2,1,0:T(8,128)(2,1)S(1)} %get-tuple-element.45, s32[1024]{0:T(1024)} %copy-done.17), kind=kCustom, calls=%fused_computation.5 | custom fusion | bytes 1572872 | tf_op jit(solution)/shard_map/gather | solution.py:50
  90.5 2.2 %copy.48 = bf16[2,128,1536]{1,0,2:T(2,128)(2,1)S(1)} copy(bf16[2,128,1536]{2,1,0:T(8,128)(2,1)} %gather_fusion.6) | data formatting | bytes 1572864 | tf_op jit(solution)/shard_map/gather | solution.py:51
  92.8 1.4 %reshape.925 = bf16[256,12,128]{0,2,1:T(8,128)(2,1)} reshape(bf16[2,128,1536]{1,0,2:T(2,128)(2,1)S(1)} %copy.48) | data formatting | bytes 1572864 | tf_op jit(solution)/shard_map/reshape.85
  94.7 2.3 %copy.44 = bf16[2,128,1536]{1,0,2:T(2,128)(2,1)S(1)} copy(bf16[2,128,1536]{2,1,0:T(8,128)(2,1)} %gather_fusion.4) | data formatting | bytes 1572864 | tf_op jit(solution)/shard_map/gather | solution.py:51
  97.0 1.4 %reshape.921 = bf16[256,12,128]{0,2,1:T(8,128)(2,1)} reshape(bf16[2,128,1536]{1,0,2:T(2,128)(2,1)S(1)} %copy.44) | data formatting | bytes 1572864 | tf_op jit(solution)/shard_map/reshape.68
  104.9 1.8 %fusion.84 = (f32[1,128,1536]{1,2,0:T(8,128)}, f32[1,128,1536]{1,2,0:T(8,128)S(1)}) fusion(f32[1536]{0:T(1024)S(1)} %copy-done.13, f32[1536]{0:T(1024)S(1)} %copy-done.12, f32[128]{0:T(128)S(1)} %add_rsqrt_fusion.4, f32[128]{0:T(128)S(1)} %broadcast_multiply_fusion, f32[1,128,12,128]{1,3,2,0:T(8,128)S(1)} %fusion.10, f32[1536]{0:T(1024)S(1)} %get-tuple-element.74, ...), kind=kLoop, calls=%fused_computation.175 | loop fusion | flops 1769472 | bytes 2771969 | tf_op jit(solution)/shard_map/mul | solution.py:48
  110.6 1.6 %collective-permute-start.5 = (bf16[1,128,1536]{1,2,0:T(8,128)(2,1)S(1)}, bf16[1,128,1536]{1,2,0:T(8,128)(2,1)S(1)}, u32[]{:S(2)}, u32[]{:S(2)}) collective-permute-start(bf16[1,128,1536]{1,2,0:T(8,128)(2,1)S(1)} %fusion.23), channel_id=1, source_target_pairs={{0,2},{2,4},{4,6},{6,8},{8,10},{10,12},{12,14},{14,0},{1,3},{3,5},... | collective-permute-start | bytes 1179656 | tf_op jit(solution)/shard_map/ppermute | solution.py:37
  112.3 9.1 %collective-permute-done.5 = bf16[1,128,1536]{1,2,0:T(8,128)(2,1)S(1)} collective-permute-done((bf16[1,128,1536]{1,2,0:T(8,128)(2,1)S(1)}, bf16[1,128,1536]{1,2,0:T(8,128)(2,1)S(1)}, u32[]{:S(2)}, u32[]{:S(2)}) %collective-permute-start.5) | collective-permute-done | bytes 393248 | tf_op jit(solution)/shard_map/ppermute | solution.py:37
  (101 shorter events, 30.0 us)
Async XLA Ops:
  0.0 31.5 %collective-permute-start.1 = (bf16[2,2,1,256,1536]{4,3,2,1,0:T(8,128)(2,1)}, bf16[2,2,1,256,1536]{4,3,2,1,0:T(8,128)(2,1)}, u32[]{:S(2)}, u32[]{:S(2)}) collective-permute-start(bf16[2,2,1,256,1536]{4,3,2,1,0:T(8,128)(2,1)} %bitcast.236), channel_id=1, source_target_pairs={{1,0},{3,2},{5,4},{7,6},{9,8},{11,10},{13,12},{15,14},{17,16},{19,... | collective-permute-start | bytes 9437192 | tf_op jit(solution)/shard_map/ppermute | solution.py:30
  1.3 30.2 %collective-permute-start = (bf16[2,2,1,256,1536]{4,3,2,1,0:T(8,128)(2,1)}, bf16[2,2,1,256,1536]{4,3,2,1,0:T(8,128)(2,1)}, u32[]{:S(2)}, u32[]{:S(2)}) collective-permute-start(bf16[2,2,1,256,1536]{4,3,2,1,0:T(8,128)(2,1)} %bitcast.237), channel_id=1, source_target_pairs={{0,1},{2,3},{4,5},{6,7},{8,9},{10,11},{12,13},{14,15},{16,17},{18,... | collective-permute-start | bytes 9437192 | tf_op jit(solution)/shard_map/ppermute | solution.py:29
  7.6 19.0 %collective-permute-start.4 = (s32[1]{0:T(128)}, s32[1]{0:T(128)}, u32[]{:S(2)}, u32[]{:S(2)}) collective-permute-start(s32[1]{0:T(128)} %param.9), channel_id=1, source_target_pairs={{0,2},{2,4},{4,6},{6,8},{8,10},{10,12},{12,14},{14,0},{1,3},{3,5},... | collective-permute-start | bytes 20 | tf_op jit(solution)/shard_map/ppermute | solution.py:37
  10.6 16.6 %collective-permute-start.3 = (s32[1]{0:T(128)}, s32[1]{0:T(128)}, u32[]{:S(2)}, u32[]{:S(2)}) collective-permute-start(s32[1]{0:T(128)} %param.10), channel_id=1, source_target_pairs={{0,2},{2,4},{4,6},{6,8},{8,10},{10,12},{12,14},{14,0},{1,3},{3,5},... | collective-permute-start | bytes 20 | tf_op jit(solution)/shard_map/ppermute | solution.py:37
  19.7 1.2 copy-start.6
  19.7 1.2 copy-start.8
  20.9 10.6 %copy-start = (bf16[1,2,2,256,1536]{4,3,2,1,0:T(8,128)(2,1)S(1)}, bf16[1,2,2,256,1536]{4,3,2,1,0:T(8,128)(2,1)}, u32[]{:S(2)}) copy-start(bf16[1,2,2,256,1536]{4,3,2,1,0:T(8,128)(2,1)} %param.15) | copy-start | bytes 9437188
  67.1 1.1 copy-start.5
  68.7 0.7 copy-start.10
  68.7 0.7 copy-start.11
  74.7 1.1 copy-start.3
  75.8 0.7 copy-start.9
  76.3 2.9 %copy-start.20 = (s32[2]{0:T(128)S(1)}, s32[2]{0:T(128)}, u32[]{:S(2)}) copy-start(s32[2]{0:T(128)} %get-tuple-element.68) | copy-start | bytes 28
  76.3 2.9 %copy-start.7 = (bf16[3,3,1536]{2,1,0:T(4,128)(2,1)S(1)}, bf16[3,3,1536]{2,1,0:T(4,128)(2,1)}, u32[]{:S(2)}) copy-start(bf16[3,3,1536]{2,1,0:T(4,128)(2,1)} %copy-done.6) | copy-start | bytes 82948
  76.3 3.1 %copy-start.16 = (f32[1,3,1536]{2,0,1:T(1,128)S(1)}, f32[1,3,1536]{2,0,1:T(1,128)}, u32[]{:S(2)}) copy-start(f32[1,3,1536]{2,0,1:T(1,128)} %fusion.44) | copy-start | bytes 55300
  77.7 21.3 %collective-permute-start.2 = (bf16[1,128,1536]{1,2,0:T(8,128)(2,1)}, bf16[1,128,1536]{1,2,0:T(8,128)(2,1)S(1)}, u32[]{:S(2)}, u32[]{:S(2)}) collective-permute-start(bf16[1,128,1536]{1,2,0:T(8,128)(2,1)} %fusion.22), channel_id=1, source_target_pairs={{0,2},{2,4},{4,6},{6,8},{8,10},{10,12},{12,14},{14,0},{1,3},{3,5},... | collective-permute-start | bytes 1179656 | tf_op jit(solution)/shard_map/ppermute | solution.py:37
  79.2 0.8 copy-start.17
  94.7 3.8 %copy-start.1 = (bf16[2,128,1536]{2,1,0:T(8,128)(2,1)S(1)}, bf16[2,128,1536]{2,1,0:T(8,128)(2,1)}, u32[]{:S(2)}) copy-start(bf16[2,128,1536]{2,1,0:T(8,128)(2,1)} %gather_fusion.5) | copy-start | bytes 2359300
  98.4 1.0 copy-start.14
  98.4 1.0 copy-start.15
  99.2 2.8 %copy-start.19 = (f32[128]{0:T(128)S(1)}, f32[128]{0:T(128)}, u32[]{:S(2)}) copy-start(f32[128]{0:T(128)} %get-tuple-element.56) | copy-start | bytes 1540
  102.6 1.1 copy-start.4
  104.2 0.7 copy-start.12
  104.2 0.7 copy-start.13
  104.9 3.0 %copy-start.18 = (f32[128]{0:T(128)S(1)}, f32[128]{0:T(128)}, u32[]{:S(2)}) copy-start(f32[128]{0:T(128)} %get-tuple-element.55) | copy-start | bytes 1540
  108.5 1.1 copy-start.2
  110.6 10.7 %collective-permute-start.5 = (bf16[1,128,1536]{1,2,0:T(8,128)(2,1)S(1)}, bf16[1,128,1536]{1,2,0:T(8,128)(2,1)S(1)}, u32[]{:S(2)}, u32[]{:S(2)}) collective-permute-start(bf16[1,128,1536]{1,2,0:T(8,128)(2,1)S(1)} %fusion.23), channel_id=1, source_target_pairs={{0,2},{2,4},{4,6},{6,8},{8,10},{10,12},{12,14},{14,0},{1,3},{3,5},... | collective-permute-start | bytes 1179656 | tf_op jit(solution)/shard_map/ppermute | solution.py:37
where the time goes:
time: 124 us; the launch traced here: 122 us
  local copies, waits for them, and re-layouts  54.9 us (44%)
  other arithmetic  28.1 us (23%)
  starting transfers between devices  15.2 us (12%)
  waiting for transfers between devices  9.1 us (7%)
  matrix products  9.07 us (7%)
  between operations  5.86 us (5%)
    gather x8, local copies, waits for them, and re-layouts, attend(): value_tiles[tile_choice].reshape(batch_size, NB * TILE, HEADS, HDIM)  22.1 us
    another operation x8, local copies, waits for them, and re-layouts  9.75 us
    ppermute x4, waiting for transfers between devices, from_behind(): lax.ppermute(x, axis, [(i, (i + by) % devices) for i in range(devices)])  9.1 us
    ppermute x4, starting transfers between devices, from_behind(): lax.ppermute(x, axis, [(i, (i + by) % devices) for i in range(devices)])  7.64 us
    gather x4, local copies, waits for them, and re-layouts, attend(): key_tiles[tile_choice].reshape(batch_size, NB * TILE, HEADS, HDIM)  7.09 us
    concatenate x1, other arithmetic, extended_2(): x = jnp.concatenate([before, x, after], axis=dim)  6.96 us
    mul x4, other arithmetic, attend(): head_rms = jnp.mean(heads_in * heads_in, axis=-1, keepdims=True)  6.79 us
    squeeze x1, local copies, waits for them, and re-layouts, run_slots(): extended[slot_index, 0]  6.49 us
  transfers between devices with their start and end apart: 6, of which 1 were waited for; matrix products, arithmetic and copies ran while one was open for 27% of the time, Pallas kernels for 0%

commit v1 on v0

v1 whole, which is shorter than its diff:
```python
import functools
import math
import jax
import jax.numpy as jnp
from jax import lax
from jax.experimental import pallas as pl
from jax.experimental.pallas import tpu as pltpu
from jax.sharding import PartitionSpec as P

TICKS = 2
EPSILON = 1e-06


def from_behind(x, axis, by):
    devices = lax.axis_size(axis)
    return lax.ppermute(x, axis, [(i, (i + by) % devices) for i in range(devices)])


def section_kernel(
    tick,
    cycle_size,
    bounds_ref,
    neighbours_ref,
    position_ref,
    step_ref,
    patch_ref,
    modulation_ref,
    gain_ref,
    own_ref,
    other_ref,
    out_ref,
    state_ref,
    query_ref,
):
    width = patch_ref.shape[1]
    layers, head_dim = gain_ref.shape
    heads = width // head_dim
    slots = own_ref.shape[0]
    tile = head_dim
    tile = own_ref.shape[2] // (neighbours_ref.shape[1] // 2)
    slab = own_ref.shape[2] // tile
    pipe = bounds_ref.shape[0] - 1
    device = lax.axis_index("segment")
    space = lax.axis_index("space")
    section = lax.rem(device, pipe)
    root = lax.rem(device - tick + cycle_size, cycle_size)
    row = step_ref[0] + jnp.where(lax.rem(root, pipe) + tick >= pipe, 1, 0)
    first_layer = bounds_ref[section]
    layer_count = bounds_ref[section + 1] - first_layer
    query_tile = space * slab + position_ref[0]
    own_row = pl.multiple_of(lax.rem(neighbours_ref[0, query_tile], slab) * tile, tile)
    other_row = pl.multiple_of(lax.rem(neighbours_ref[1, query_tile], slab) * tile, tile)
    scale = head_dim ** -0.5 * math.log2(math.e)

    state_ref[...] = patch_ref[...].astype(jnp.float32)

    def layer(slot):
        layer_now = jnp.minimum(first_layer + slot, layers - 1)
        mods = modulation_ref[row, layer_now].astype(jnp.float32)
        gain = gain_ref[pl.ds(layer_now, 1), :]
        state = state_ref[...]
        middle = jnp.mean(state, axis=-1, keepdims=True)
        centred = state - middle
        spread = jnp.mean(centred * centred, axis=-1, keepdims=True)
        normed = centred * lax.rsqrt(spread + EPSILON)
        shifted = normed * (1.0 + mods[1:2, :]) + mods[0:1, :]
        for head in range(heads):
            cols = slice(head * head_dim, (head + 1) * head_dim)
            part = shifted[:, cols]
            power = jnp.mean(part * part, axis=-1, keepdims=True)
            query_ref[:, cols] = (part * lax.rsqrt(power + EPSILON) * gain).astype(jnp.bfloat16)
        for head in range(heads):
            cols = slice(head * head_dim, (head + 1) * head_dim)
            keys = jnp.concatenate(
                [own_ref[slot, 0, pl.ds(own_row, tile), cols], other_ref[slot, 0, pl.ds(other_row, tile), cols]]
            )
            values = jnp.concatenate(
                [own_ref[slot, 1, pl.ds(own_row, tile), cols], other_ref[slot, 1, pl.ds(other_row, tile), cols]]
            )
            scores = lax.dot_general(
                query_ref[:, cols], keys, (((1,), (1,)), ((), ())), preferred_element_type=jnp.float32
            )
            top = jnp.max(scores, axis=-1, keepdims=True)
            powers = jnp.exp2((scores - top) * scale)
            total = jnp.sum(powers, axis=-1, keepdims=True)
            blended = jnp.dot(powers.astype(jnp.bfloat16), values, preferred_element_type=jnp.float32)
            state_ref[:, cols] += mods[2:3, cols] * (blended / total)

    layer(0)
    for slot in range(1, slots):
        pl.when(layer_count > slot)(functools.partial(layer, slot))
    out_ref[...] = state_ref[...].astype(jnp.bfloat16)


def run_section(tick, cycle_size, patch, position, step, bounds, neighbours, modulation, gains, own, other):
    rows, width = patch.shape
    smem = pl.BlockSpec(memory_space=pltpu.SMEM)
    vmem = pl.BlockSpec(memory_space=pltpu.VMEM)
    pin = lambda x: pltpu.with_memory_space_constraint(x, pltpu.VMEM)
    return pl.pallas_call(
        functools.partial(section_kernel, tick, cycle_size),
        out_shape=jax.ShapeDtypeStruct((rows, width), jnp.bfloat16),
        in_specs=[smem] * 4 + [vmem] * 5,
        out_specs=vmem,
        scratch_shapes=[
            pltpu.VMEM((rows, width), jnp.float32),
            pltpu.VMEM((rows, width), jnp.bfloat16),
        ],
        compiler_params=pltpu.CompilerParams(vmem_limit_bytes=16 << 20),
        cost_estimate=pl.CostEstimate(flops=800_000_000, bytes_accessed=8_000_000, transcendentals=800_000),
        name="section",
    )(bounds, neighbours, position, step, patch, pin(modulation), pin(gains), pin(own), pin(other))


def per_device(
    patches, positions, timesteps, section_bounds, tile_neighbours, modulation, query_gain, stale_kv
):
    own = stale_kv[0]
    other = from_behind(own, "space", 1)
    cycle_size = lax.axis_size("segment")
    neighbours = tile_neighbours.T
    holding = patches[0]
    position, step = positions, timesteps
    for tick in range(TICKS):
        if tick > 0:
            position, step = from_behind((position, step), "segment", 1)
        holding = run_section(
            tick, cycle_size, holding, position, step, section_bounds, neighbours, modulation, query_gain, own, other
        )
        holding = from_behind(holding, "segment", 1)
    return holding[None]


def solution(mesh):
    placed = (
        P(("groups", "segment"), "space", None),
        P(("groups", "segment")),
        P(("groups", "segment")),
        P(),
        P(),
        P("groups", None, None, None),
        P(),
        P(("groups", "segment"), None, None, "space", None),
    )
    return jax.shard_map(
        per_device,
        mesh=mesh,
        in_specs=placed,
        out_specs=P(("groups", "segment"), "space", None),
        check_vma=False,
    )
```

time: 124 us -> 49 us (0.40)
  local copies, waits for them, and re-layouts: 54.9 us -> 6.68 us
  other arithmetic: 28.1 us -> 0 us
  waiting for transfers between devices: 9.1 us -> 25.6 us
  matrix products: 9.07 us -> 0 us
  starting transfers between devices: 15.2 us -> 6.49 us
  Pallas kernels: 0 us -> 7.92 us
  between operations: 5.86 us -> 1.34 us
    gather x13 -> x0, local copies, waits for them, and re-layouts: 30.1 us -> none  [the longest x8 22.1 us: attend(): value_tiles[tile_choice].reshape(batch_size, NB * TILE, HEADS, HDIM)]
    ppermute x4 -> x5, waiting for transfers between devices: 9.1 us -> 25.6 us  [from_behind(): lax.ppermute(x, axis, [(i, (i + by) % devices) for i in range(devices)])]
    another operation x8 -> x0, local copies, waits for them, and re-layouts: 9.75 us -> none
    reduce_sum x16 -> x0, other arithmetic: 9.41 us -> none  [the longest x4 5.33 us: attend(): head_rms = jnp.mean(heads_in * heads_in, axis=-1, keepdims=True)]
    dot_general x12 -> x0, matrix products: 9.07 us -> none  [the longest x4 5.23 us: attend(): jnp.einsum('bqhd,bkhd->bhqk', queries, key_rows, preferred_element_type=j...]
    pallas_call x0 -> x2, Pallas kernels: none -> 7.92 us  [run_section(): pl.pallas_call(functools.partial(section_kernel, tick, cycle_size), out_s...]
    ppermute x2 -> x0, starting transfers between devices: 7.61 us -> none  [the longest x1 6.33 us: extended_2(): before = lax.ppermute(last, axis, up)]
    squeeze x2 -> x0, local copies, waits for them, and re-layouts: 7.31 us -> none  [the longest x1 6.49 us: run_slots(): extended[slot_index, 0]]
  transfers between devices with their start and end apart: 6 -> 5, of which waited for: 1 -> 4; matrix products, arithmetic and copies ran while one was open for 27% -> 0% of each run, Pallas kernels for 0% -> 0%
where the time goes in v1:
time: 49 us; the launch traced here: 48.1 us
  waiting for transfers between devices  25.6 us (52%)
  Pallas kernels  7.92 us (16%)
  local copies, waits for them, and re-layouts  6.68 us (14%)
  starting transfers between devices  6.49 us (13%)
  between operations  1.34 us (3%)
    ppermute x5, waiting for transfers between devices, from_behind(): lax.ppermute(x, axis, [(i, (i + by) % devices) for i in range(devices)])  25.6 us
    pallas_call x2, Pallas kernels, run_section(): pl.pallas_call(functools.partial(section_kernel, tick, cycle_size), out_s...  7.92 us
    unnamed x17, local copies, waits for them, and re-layouts  6.68 us
    ppermute x5, starting transfers between devices, from_behind(): lax.ppermute(x, axis, [(i, (i + by) % devices) for i in range(devices)])  6.49 us
  transfers between devices with their start and end apart: 5, of which 4 were waited for; matrix products, arithmetic and copies ran while one was open for 0% of the time, Pallas kernels for 0%

profile of v1, /device:TPU:0, one launch (start us, length us, event | category | flops | bytes accessed | tf_op | source)
XLA Modules:
  0.0 48.1 jit_solution(8654614756149374321)
XLA Ops:
  0.0 0.5 %collective-permute-start.2 = (bf16[2,2,256,1536]{3,2,1,0:T(8,128)(2,1)}, bf16[2,2,256,1536]{3,2,1,0:T(8,128)(2,1)S(1)}, u32[]{:S(2)}, u32[]{:S(2)}) collective-permute-start(bf16[2,2,256,1536]{3,2,1,0:T(8,128)(2,1)} %bitcast.4), channel_id=1, source_target_pairs={{0,1},{1,0},{2,3},{3,2},{4,5},{5,4},{6,7},{7,6},{8,9},{9,8},{10,11... | collective-permute-start | bytes 9437192 | tf_op jit(solution)/shard_map/ppermute | solution.py:16
  1.8 4.2 %collective-permute-done.2.other_ref = bf16[2,2,256,1536]{3,2,1,0:T(8,128)(2,1)S(1)} collective-permute-done((bf16[2,2,256,1536]{3,2,1,0:T(8,128)(2,1)}, bf16[2,2,256,1536]{3,2,1,0:T(8,128)(2,1)S(1)}, u32[]{:S(2)}, u32[]{:S(2)}) %collective-permute-start.2) | collective-permute-done | bytes 3145760 | tf_op jit(solution)/shard_map/ppermute | solution.py:16
  6.0 0.0 copy-start
  6.0 1.9 %copy-done = bf16[1,2,2,256,1536]{4,3,2,1,0:T(8,128)(2,1)S(1)} copy-done((bf16[1,2,2,256,1536]{4,3,2,1,0:T(8,128)(2,1)S(1)}, bf16[1,2,2,256,1536]{4,3,2,1,0:T(8,128)(2,1)}, u32[]{:S(2)}) %copy-start) | copy-done | bytes 3145752
  7.9 0.0 copy-start.2
  7.9 1.0 %copy-done.2 = bf16[3,12,3,1536]{3,2,1,0:T(4,128)(2,1)S(1)} copy-done((bf16[3,12,3,1536]{3,2,1,0:T(4,128)(2,1)S(1)}, bf16[3,12,3,1536]{3,2,1,0:T(4,128)(2,1)}, u32[]{:S(2)}) %copy-start.2) | copy-done | bytes 331800
  8.9 0.0 copy-start.4
  8.9 1.0 %copy-done.4 = bf16[1,128,1536]{2,1,0:T(8,128)(2,1)S(1)} copy-done((bf16[1,128,1536]{2,1,0:T(8,128)(2,1)S(1)}, bf16[1,128,1536]{2,1,0:T(8,128)(2,1)}, u32[]{:S(2)}) %copy-start.4) | copy-done | bytes 393240
  9.9 0.0 copy-start.5
  9.9 0.7 %copy-done.5 = f32[12,128]{1,0:T(8,128)S(1)} copy-done((f32[12,128]{1,0:T(8,128)S(1)}, f32[12,128]{1,0:T(8,128)}, u32[]{:S(2)}) %copy-start.5) | copy-done | bytes 6168
  10.6 0.0 copy-start.6
  10.6 0.7 %copy-done.6 = s32[4,2]{0,1:T(2,128)S(1)} copy-done((s32[4,2]{0,1:T(2,128)S(1)}, s32[4,2]{0,1:T(2,128)}, u32[]{:S(2)}) %copy-start.6) | copy-done | bytes 56
  11.3 0.0 copy-start.7
  11.3 0.7 %copy-done.7 = s32[9]{0:T(128)S(1)} copy-done((s32[9]{0:T(128)S(1)}, s32[9]{0:T(128)}, u32[]{:S(2)}) %copy-start.7) | copy-done | bytes 60
  11.9 0.0 copy-start.1
  11.9 0.0 copy-start.3
  11.9 3.4 %section.2 = bf16[128,1536]{1,0:T(8,128)(2,1)S(1)} custom-call(s32[9]{0:T(128)S(1)} %copy-done.7, s32[2,4]{1,0:T(2,128)S(1)} %bitcast.8, s32[1]{0:T(128)S(6)} %copy.10.position_ref, s32[1]{0:T(128)S(6)} %copy.11.step_ref, bf16[128,1536]{1,0:T(8,128)(2,1)S(1)} %bitcast.7, bf16[3,12,3,1536]{3,2,1,0:T(4,128)(2,1)S(1)} %copy-done.2, f32[12,128]{1,0:T(8,128)S(1)} %copy-done.5, ...), custom_call_target="tpu_custom_call" | custom-call | flops 800000000 | bytes 8000000 | tf_op jit(solution)/shard_map/section/pallas_call | solution.py:100
  15.3 1.5 %collective-permute-start.3 = (bf16[128,1536]{1,0:T(8,128)(2,1)S(1)}, bf16[128,1536]{1,0:T(8,128)(2,1)S(1)}, u32[]{:S(2)}, u32[]{:S(2)}) collective-permute-start(bf16[128,1536]{1,0:T(8,128)(2,1)S(1)} %section.2), channel_id=1, source_target_pairs={{0,2},{2,4},{4,6},{6,8},{8,10},{10,12},{12,14},{14,0},{1,3},{3,5},... | collective-permute-start | bytes 1179656 | tf_op jit(solution)/shard_map/ppermute | solution.py:16
  16.8 2.9 %collective-permute-start = (s32[1]{0:T(128)}, s32[1]{0:T(128)}, u32[]{:S(2)}, u32[]{:S(2)}) collective-permute-start(s32[1]{0:T(128)} %param.9), channel_id=1, source_target_pairs={{0,2},{2,4},{4,6},{6,8},{8,10},{10,12},{12,14},{14,0},{1,3},{3,5},... | collective-permute-start | bytes 20 | tf_op jit(solution)/shard_map/ppermute | solution.py:16
  19.7 1.5 %collective-permute-start.1 = (s32[1]{0:T(128)}, s32[1]{0:T(128)}, u32[]{:S(2)}, u32[]{:S(2)}) collective-permute-start(s32[1]{0:T(128)} %param.10), channel_id=1, source_target_pairs={{0,2},{2,4},{4,6},{6,8},{8,10},{10,12},{12,14},{14,0},{1,3},{3,5},... | collective-permute-start | bytes 20 | tf_op jit(solution)/shard_map/ppermute | solution.py:16
  21.2 8.3 %collective-permute-done.position_ref = s32[1]{0:T(128)} collective-permute-done((s32[1]{0:T(128)}, s32[1]{0:T(128)}, u32[]{:S(2)}, u32[]{:S(2)}) %collective-permute-start) | collective-permute-done | bytes 36 | tf_op jit(solution)/shard_map/ppermute | solution.py:16
  29.6 0.1 collective-permute-done.1.step_ref
  29.7 0.0 collective-permute-done.3.patch_ref
  29.7 0.0 copy-done.1
  29.7 0.0 copy-done.3
  29.7 4.6 %section.3 = bf16[128,1536]{1,0:T(8,128)(2,1)S(1)} custom-call(s32[9]{0:T(128)S(1)} %copy-done.7, s32[2,4]{1,0:T(2,128)S(1)} %bitcast.9, s32[1]{0:T(128)} %collective-permute-done.position_ref, s32[1]{0:T(128)} %collective-permute-done.1.step_ref, bf16[128,1536]{1,0:T(8,128)(2,1)S(1)} %collective-permute-done.3.patch_ref, ...), custom_call_target="tpu_custom_call" | custom-call | flops 800000000 | bytes 8000000 | tf_op jit(solution)/shard_map/section/pallas_call | solution.py:100
  34.2 0.1 collective-permute-start.4
  34.3 13.0 %collective-permute-done.4 = bf16[128,1536]{1,0:T(8,128)(2,1)S(1)} collective-permute-done((bf16[128,1536]{1,0:T(8,128)(2,1)S(1)}, bf16[128,1536]{1,0:T(8,128)(2,1)S(1)}, u32[]{:S(2)}, u32[]{:S(2)}) %collective-permute-start.4) | collective-permute-done | bytes 393248 | tf_op jit(solution)/shard_map/ppermute | solution.py:16
  47.3 0.7 %copy.12 = bf16[1,128,1536]{2,1,0:T(8,128)(2,1)} copy(bf16[1,128,1536]{2,1,0:T(8,128)(2,1)S(1)} %bitcast.10) | data formatting | bytes 786432
Async XLA Ops:
  0.0 6.0 %collective-permute-start.2 = (bf16[2,2,256,1536]{3,2,1,0:T(8,128)(2,1)}, bf16[2,2,256,1536]{3,2,1,0:T(8,128)(2,1)S(1)}, u32[]{:S(2)}, u32[]{:S(2)}) collective-permute-start(bf16[2,2,256,1536]{3,2,1,0:T(8,128)(2,1)} %bitcast.4), channel_id=1, source_target_pairs={{0,1},{1,0},{2,3},{3,2},{4,5},{5,4},{6,7},{7,6},{8,9},{9,8},{10,11... | collective-permute-start | bytes 9437192 | tf_op jit(solution)/shard_map/ppermute | solution.py:16
  6.0 1.9 %copy-start = (bf16[1,2,2,256,1536]{4,3,2,1,0:T(8,128)(2,1)S(1)}, bf16[1,2,2,256,1536]{4,3,2,1,0:T(8,128)(2,1)}, u32[]{:S(2)}) copy-start(bf16[1,2,2,256,1536]{4,3,2,1,0:T(8,128)(2,1)} %param.15) | copy-start | bytes 9437188
  7.9 1.0 %copy-start.2 = (bf16[3,12,3,1536]{3,2,1,0:T(4,128)(2,1)S(1)}, bf16[3,12,3,1536]{3,2,1,0:T(4,128)(2,1)}, u32[]{:S(2)}) copy-start(bf16[3,12,3,1536]{3,2,1,0:T(4,128)(2,1)} %modulation_ref.3) | copy-start | bytes 995332
  8.9 1.0 %copy-start.4 = (bf16[1,128,1536]{2,1,0:T(8,128)(2,1)S(1)}, bf16[1,128,1536]{2,1,0:T(8,128)(2,1)}, u32[]{:S(2)}) copy-start(bf16[1,128,1536]{2,1,0:T(8,128)(2,1)} %param.8) | copy-start | bytes 1179652
  9.9 0.7 %copy-start.5 = (f32[12,128]{1,0:T(8,128)S(1)}, f32[12,128]{1,0:T(8,128)}, u32[]{:S(2)}) copy-start(f32[12,128]{1,0:T(8,128)} %gain_ref.3) | copy-start | bytes 18436
  10.6 0.7 %copy-start.6 = (s32[4,2]{0,1:T(2,128)S(1)}, s32[4,2]{0,1:T(2,128)}, u32[]{:S(2)}) copy-start(s32[4,2]{0,1:T(2,128)} %param.12) | copy-start | bytes 100
  11.3 0.7 %copy-start.7 = (s32[9]{0:T(128)S(1)}, s32[9]{0:T(128)}, u32[]{:S(2)}) copy-start(s32[9]{0:T(128)} %bounds_ref.3) | copy-start | bytes 112
  11.9 17.7 %copy-start.1 = (bf16[1,2,2,256,1536]{4,3,2,1,0:T(8,128)(2,1)S(1)}, bf16[1,2,2,256,1536]{4,3,2,1,0:T(8,128)(2,1)}, u32[]{:S(2)}) copy-start(bf16[1,2,2,256,1536]{4,3,2,1,0:T(8,128)(2,1)} %param.15) | copy-start | bytes 9437188
  11.9 17.7 %copy-start.3 = (bf16[3,12,3,1536]{3,2,1,0:T(4,128)(2,1)S(1)}, bf16[3,12,3,1536]{3,2,1,0:T(4,128)(2,1)}, u32[]{:S(2)}) copy-start(bf16[3,12,3,1536]{3,2,1,0:T(4,128)(2,1)} %modulation_ref.3) | copy-start | bytes 995332
  15.3 14.4 %collective-permute-start.3 = (bf16[128,1536]{1,0:T(8,128)(2,1)S(1)}, bf16[128,1536]{1,0:T(8,128)(2,1)S(1)}, u32[]{:S(2)}, u32[]{:S(2)}) collective-permute-start(bf16[128,1536]{1,0:T(8,128)(2,1)S(1)} %section.2), channel_id=1, source_target_pairs={{0,2},{2,4},{4,6},{6,8},{8,10},{10,12},{12,14},{14,0},{1,3},{3,5},... | collective-permute-start | bytes 1179656 | tf_op jit(solution)/shard_map/ppermute | solution.py:16
  16.8 12.8 %collective-permute-start = (s32[1]{0:T(128)}, s32[1]{0:T(128)}, u32[]{:S(2)}, u32[]{:S(2)}) collective-permute-start(s32[1]{0:T(128)} %param.9), channel_id=1, source_target_pairs={{0,2},{2,4},{4,6},{6,8},{8,10},{10,12},{12,14},{14,0},{1,3},{3,5},... | collective-permute-start | bytes 20 | tf_op jit(solution)/shard_map/ppermute | solution.py:16
  19.7 9.9 %collective-permute-start.1 = (s32[1]{0:T(128)}, s32[1]{0:T(128)}, u32[]{:S(2)}, u32[]{:S(2)}) collective-permute-start(s32[1]{0:T(128)} %param.10), channel_id=1, source_target_pairs={{0,2},{2,4},{4,6},{6,8},{8,10},{10,12},{12,14},{14,0},{1,3},{3,5},... | collective-permute-start | bytes 20 | tf_op jit(solution)/shard_map/ppermute | solution.py:16
  34.2 13.1 %collective-permute-start.4 = (bf16[128,1536]{1,0:T(8,128)(2,1)S(1)}, bf16[128,1536]{1,0:T(8,128)(2,1)S(1)}, u32[]{:S(2)}, u32[]{:S(2)}) collective-permute-start(bf16[128,1536]{1,0:T(8,128)(2,1)S(1)} %section.3), channel_id=1, source_target_pairs={{0,2},{2,4},{4,6},{6,8},{8,10},{10,12},{12,14},{14,0},{1,3},{3,5},... | collective-permute-start | bytes 1179656 | tf_op jit(solution)/shard_map/ppermute | solution.py:16

commit v2 on v1

v2 whole, which is shorter than its diff:
```python
import functools
import math
import jax
import jax.numpy as jnp
from jax import lax
from jax.experimental import pallas as pl
from jax.experimental.pallas import tpu as pltpu
from jax.sharding import PartitionSpec as P

TICKS = 2
CHUNKS = 2
EPSILON = 1e-06
EXTRA = 8

SMEM = pl.BlockSpec(memory_space=pltpu.SMEM)
VMEM = pl.BlockSpec(memory_space=pltpu.VMEM)
ANY = pl.BlockSpec(memory_space=pl.ANY)


def from_behind(x, axis, by):
    devices = lax.axis_size(axis)
    return lax.ppermute(x, axis, [(i, (i + by) % devices) for i in range(devices)])


def pinned(x, space=pltpu.VMEM):
    return pltpu.with_memory_space_constraint(x, space)


def stage_kernel(
    bounds_hbm,
    neighbours_hbm,
    position_ref,
    step_ref,
    patch_ref,
    modulation_ref,
    gain_ref,
    own_ref,
    plan_ref,
    patch_out,
    modulation_out,
    gain_out,
    own_out,
    bounds_ref,
    neighbours_ref,
    sems,
):
    slots = own_ref.shape[0]
    small = [
        pltpu.make_async_copy(source, target, sems.at[3 + slots + i])
        for i, (source, target) in enumerate(
            [
                (bounds_hbm, bounds_ref),
                (neighbours_hbm, neighbours_ref),
            ]
        )
    ]
    copies = [
        pltpu.make_async_copy(patch_ref, patch_out, sems.at[0]),
        pltpu.make_async_copy(gain_ref, gain_out, sems.at[1]),
        pltpu.make_async_copy(own_ref, own_out, sems.at[2]),
    ]
    for copy in small + copies:
        copy.start()
    for copy in small:
        copy.wait()
    pipe = bounds_ref.shape[0] - 1
    layers = gain_ref.shape[0]
    device = lax.axis_index("segment")
    space = lax.axis_index("space")
    section = lax.rem(device, pipe)
    first_layer = bounds_ref[section]
    for slot in range(slots):
        layer_now = jnp.minimum(first_layer + slot, layers - 1)
        copy = pltpu.make_async_copy(modulation_ref.at[:, layer_now], modulation_out.at[slot], sems.at[3 + slot])
        copy.start()
        copies.append(copy)
    slab = neighbours_ref.shape[1] // 2
    plan_ref[0] = first_layer
    plan_ref[1] = bounds_ref[section + 1] - first_layer
    plan_ref[2] = position_ref[0]
    plan_ref[3] = step_ref[0]
    for place in range(slab):
        plan_ref[4 + place] = lax.rem(neighbours_ref[0, space * slab + place], slab)
        plan_ref[4 + slab + place] = lax.rem(neighbours_ref[1, space * slab + place], slab)
    for copy in copies:
        copy.wait()


def stage(bounds, neighbours, position, step, patch, modulation, gains, own):
    slots = own.shape[0]
    plan_size = 4 + neighbours.shape[1]
    return pl.pallas_call(
        stage_kernel,
        out_shape=(
            pltpu.SMEM((plan_size,), jnp.int32),
            pltpu.VMEM(patch.shape, patch.dtype),
            pltpu.VMEM((slots, modulation.shape[0]) + modulation.shape[2:], modulation.dtype),
            pltpu.VMEM(gains.shape, gains.dtype),
            pltpu.VMEM(own.shape, own.dtype),
        ),
        in_specs=[ANY] * 2 + [SMEM] * 2 + [ANY] * 4,
        out_specs=(SMEM, VMEM, VMEM, VMEM, VMEM),
        scratch_shapes=[pltpu.SMEM(x.shape, x.dtype) for x in (bounds, neighbours)]
        + [pltpu.SemaphoreType.DMA((5 + slots,))],
        compiler_params=pltpu.CompilerParams(vmem_limit_bytes=16 << 20),
        cost_estimate=pl.CostEstimate(flops=0, bytes_accessed=7_000_000, transcendentals=0),
        name="stage",
    )(
        pinned(bounds, pltpu.HBM),
        pinned(neighbours, pltpu.HBM),
        position,
        step,
        *(pinned(x, pltpu.HBM) for x in (patch, modulation, gains, own)),
    )


def section_kernel(
    tick,
    start,
    cycle_size,
    pipe,
    plan_ref,
    patch_ref,
    modulation_ref,
    gain_ref,
    own_ref,
    other_ref,
    out_ref,
    state_ref,
):
    rows, width = state_ref.shape
    layers, head_dim = gain_ref.shape
    heads = width // head_dim
    slots = own_ref.shape[0]
    slab = (plan_ref.shape[0] - 4) // 2
    tile = own_ref.shape[2] // slab
    device = lax.axis_index("segment")
    root = lax.rem(device - tick + cycle_size, cycle_size)
    if tick == 0:
        position = plan_ref[2]
        step = plan_ref[3]
    else:
        tail = patch_ref[heads * rows : heads * rows + EXTRA, :].astype(jnp.float32)
        lanes = lax.broadcasted_iota(jnp.int32, tail.shape, 1)
        position = jnp.max(jnp.where(lanes == 0, tail, 0.0)).astype(jnp.int32)
        step = jnp.max(jnp.where(lanes == 1, tail, 0.0)).astype(jnp.int32)
    row = step + jnp.where(lax.rem(root, pipe) + tick >= pipe, 1, 0)
    first_layer = plan_ref[0]
    layer_count = plan_ref[1]
    own_row = pl.multiple_of(plan_ref[4 + position] * tile, tile)
    other_row = pl.multiple_of(plan_ref[4 + slab + position] * tile, tile)
    scale = head_dim ** -0.5 * math.log2(math.e)

    for head in range(heads):
        cols = slice(head * head_dim, (head + 1) * head_dim)
        if tick == 0:
            state_ref[:, cols] = patch_ref[start : start + rows, cols].astype(jnp.float32)
        else:
            state_ref[:, cols] = patch_ref[head * rows : (head + 1) * rows, :].astype(jnp.float32)

    def layer(slot):
        layer_now = jnp.minimum(first_layer + slot, layers - 1)
        mods = modulation_ref[slot, row].astype(jnp.float32)
        gain = gain_ref[pl.ds(layer_now, 1), :]
        blocks = [slice(head * head_dim, (head + 1) * head_dim) for head in range(heads)]

        def tiles(kind, cols):
            return jnp.concatenate(
                [
                    own_ref[slot, kind, pl.ds(own_row, tile), cols],
                    other_ref[slot, kind, pl.ds(other_row, tile), cols],
                ]
            )

        state = [state_ref[:, cols] for cols in blocks]
        middle = jnp.sum(sum(state[1:], state[0]), axis=-1, keepdims=True) / width
        centred = [part - middle for part in state]
        squares = [part * part for part in centred]
        spread = jnp.sum(sum(squares[1:], squares[0]), axis=-1, keepdims=True) / width
        sharp = lax.rsqrt(spread + EPSILON)
        shifted = [
            part * sharp * (1.0 + mods[1:2, cols]) + mods[0:1, cols] for part, cols in zip(centred, blocks)
        ]
        powers = [jnp.mean(part * part, axis=-1, keepdims=True) for part in shifted]
        queries = [
            (part * lax.rsqrt(power + EPSILON) * gain).astype(jnp.bfloat16)
            for part, power in zip(shifted, powers)
        ]
        scores = [
            lax.dot_general(
                query, tiles(0, cols), (((1,), (1,)), ((), ())), preferred_element_type=jnp.float32
            )
            for query, cols in zip(queries, blocks)
        ]
        tops = [jnp.max(part, axis=-1, keepdims=True) for part in scores]
        weights = [jnp.exp2((part - top) * scale) for part, top in zip(scores, tops)]
        totals = [jnp.sum(part, axis=-1, keepdims=True) for part in weights]
        blended = [
            jnp.dot(part.astype(jnp.bfloat16), tiles(1, cols), preferred_element_type=jnp.float32)
            for part, cols in zip(weights, blocks)
        ]
        for part, blend, total, cols in zip(state, blended, totals, blocks):
            state_ref[:, cols] = part + mods[2:3, cols] * (blend / total)

    layer(0)
    for slot in range(1, slots):
        pl.when(layer_count > slot)(functools.partial(layer, slot))

    if tick == 0:
        for head in range(heads):
            cols = slice(head * head_dim, (head + 1) * head_dim)
            out_ref[head * rows : (head + 1) * rows, :] = state_ref[:, cols].astype(out_ref.dtype)
        lanes = lax.broadcasted_iota(jnp.int32, (EXTRA, head_dim), 1)
        tail = jnp.where(lanes == 0, position, jnp.where(lanes == 1, step, 0))
        out_ref[heads * rows : heads * rows + EXTRA, :] = tail.astype(jnp.float32).astype(out_ref.dtype)
    else:
        out_ref[...] = state_ref[...].astype(out_ref.dtype)


def run_section(tick, start, rows, cycle_size, pipe, width, plan, patch, modulation, gains, own, other):
    heads = width // gains.shape[1]
    shape = (heads * rows + EXTRA, gains.shape[1]) if tick == 0 else (rows, width)
    return pl.pallas_call(
        functools.partial(section_kernel, tick, start, cycle_size, pipe),
        out_shape=pltpu.VMEM(shape, jnp.bfloat16),
        in_specs=[SMEM] + [VMEM] * 5,
        out_specs=VMEM,
        scratch_shapes=[pltpu.VMEM((rows, width), jnp.float32)],
        compiler_params=pltpu.CompilerParams(vmem_limit_bytes=16 << 20),
        cost_estimate=pl.CostEstimate(flops=400_000_000, bytes_accessed=8_000_000, transcendentals=800_000),
        name=f"section_{tick}_{start}",
    )(plan, pinned(patch), pinned(modulation), pinned(gains), pinned(own), pinned(other))


def per_device(
    patches, positions, timesteps, section_bounds, tile_neighbours, modulation, query_gain, stale_kv
):
    own_hbm = stale_kv[0]
    other = from_behind(own_hbm, "space", 1)
    cycle_size = lax.axis_size("segment")
    pipe = section_bounds.shape[0] - 1
    tokens, width = patches.shape[1:]
    plan, patch, mods, gains, own = stage(
        section_bounds, tile_neighbours.T, positions, timesteps, patches[0], modulation, query_gain, own_hbm
    )
    rows = tokens // CHUNKS
    pieces = [patch] * CHUNKS
    for tick in range(TICKS):
        pieces = [
            from_behind(
                run_section(
                    tick, chunk * rows, rows, cycle_size, pipe, width, plan, piece, mods, gains, own, other
                ),
                "segment",
                1,
            )
            for chunk, piece in enumerate(pieces)
        ]
    return jnp.concatenate(pieces)[None]


def solution(mesh):
    placed = (
        P(("groups", "segment"), "space", None),
        P(("groups", "segment")),
        P(("groups", "segment")),
        P(),
        P(),
        P("groups", None, None, None),
        P(),
        P(("groups", "segment"), None, None, "space", None),
    )
    return jax.shard_map(
        per_device,
        mesh=mesh,
        in_specs=placed,
        out_specs=P(("groups", "segment"), "space", None),
        check_vma=False,
    )
```

time: 49 us -> 34.2 us (0.70); the launches traced: 48.1 us -> 34.1 us
  waiting for transfers between devices: 25.6 us -> 18.1 us
  local copies, waits for them, and re-layouts: 6.68 us -> 0 us
  starting transfers between devices: 6.49 us -> 4.32 us
  Pallas kernels: 7.92 us -> 9.48 us
  other arithmetic: 0 us -> 0.77 us
    ppermute x5, waiting for transfers between devices: 25.6 us -> 18.1 us  [from_behind(): lax.ppermute(x, axis, [(i, (i + by) % devices) for i in range(devices)])]
    unnamed x17 -> x0, local copies, waits for them, and re-layouts: 6.68 us -> none
    ppermute x5, starting transfers between devices: 6.49 us -> 4.32 us  [from_behind(): lax.ppermute(x, axis, [(i, (i + by) % devices) for i in range(devices)])]
    pallas_call x2 -> x5, Pallas kernels: 7.92 us -> 9.48 us  [the longest x4 7.37 us: run_section(): pl.pallas_call(functools.partial(section_kernel, tick, start, cycle_size,...]
    broadcast_in_dim x0 -> x1, other arithmetic: none -> 0.77 us  [per_device(): return jnp.concatenate(pieces)[None]]
  transfers between devices with their start and end apart: 5 -> 5, of which waited for: 4 -> 5; matrix products, arithmetic and copies ran while one was open for 0% -> 0% of each run, Pallas kernels for 0% -> 22%
where the time goes in v2:
time: 34.2 us; the launch traced here: 34.1 us
  waiting for transfers between devices  18.1 us (53%)
  Pallas kernels  9.48 us (28%)
  starting transfers between devices  4.32 us (13%)
  between operations  1.35 us (4%)
  other arithmetic  0.77 us (2%)
    ppermute x5, waiting for transfers between devices, from_behind(): lax.ppermute(x, axis, [(i, (i + by) % devices) for i in range(devices)])  18.1 us
    pallas_call x4, Pallas kernels, run_section(): pl.pallas_call(functools.partial(section_kernel, tick, start, cycle_size,...  7.37 us
    ppermute x5, starting transfers between devices, from_behind(): lax.ppermute(x, axis, [(i, (i + by) % devices) for i in range(devices)])  4.32 us
    pallas_call x1, Pallas kernels, stage(): pl.pallas_call(stage_kernel, out_shape=(pltpu.SMEM((plan_size,), jnp.int3...  2.11 us
    broadcast_in_dim x1, other arithmetic, per_device(): return jnp.concatenate(pieces)[None]  0.77 us
  transfers between devices with their start and end apart: 5, of which 5 were waited for; matrix products, arithmetic and copies ran while one was open for 0% of the time, Pallas kernels for 22%

profile of v2, /device:TPU:0, one launch (start us, length us, event | category | flops | bytes accessed | tf_op | source)
XLA Modules:
  0.0 34.1 jit_solution(10723673478187787873)
XLA Ops:
  0.0 0.5 %collective-permute-start = (bf16[2,2,256,1536]{3,2,1,0:T(8,128)(2,1)}, bf16[2,2,256,1536]{3,2,1,0:T(8,128)(2,1)S(1)}, u32[]{:S(2)}, u32[]{:S(2)}) collective-permute-start(bf16[2,2,256,1536]{3,2,1,0:T(8,128)(2,1)} %bitcast.5), channel_id=1, source_target_pairs={{0,1},{1,0},{2,3},{3,2},{4,5},{5,4},{6,7},{7,6},{8,9},{9,8},{10,11... | collective-permute-start | bytes 9437192 | tf_op jit(solution)/shard_map/ppermute | solution.py:22
  1.8 2.1 %stage.1 = (s32[8]{0:T(128)S(4)}, bf16[128,1536]{1,0:T(8,128)(2,1)S(1)}, bf16[2,3,3,1536]{3,2,1,0:T(4,128)(2,1)S(1)}, f32[12,128]{1,0:T(8,128)S(1)}, bf16[2,2,256,1536]{3,2,1,0:T(8,128)(2,1)S(1)}) custom-call(s32[9]{0:T(128)} %bounds_hbm.1, s32[2,4]{1,0:T(2,128)} %bitcast.8, s32[1]{0:T(128)S(6)} %copy.9.position_ref, s32[1]{0:T(128)S(6)} %copy.10.step_ref, ...), custom_call_target="tpu_custom_call" | custom-call | bytes 7000000 | tf_op jit(solution)/shard_map/stage/pallas_call | solution.py:92
  3.9 2.1 %collective-permute-done.other_ref = bf16[2,2,256,1536]{3,2,1,0:T(8,128)(2,1)S(1)} collective-permute-done((bf16[2,2,256,1536]{3,2,1,0:T(8,128)(2,1)}, bf16[2,2,256,1536]{3,2,1,0:T(8,128)(2,1)S(1)}, u32[]{:S(2)}, u32[]{:S(2)}) %collective-permute-start) | collective-permute-done | bytes 3145760 | tf_op jit(solution)/shard_map/ppermute | solution.py:22
  6.0 1.8 %section_0_0.1 = bf16[776,128]{1,0:T(8,128)(2,1)S(1)} custom-call(s32[8]{0:T(128)S(4)} %get-tuple-element.10.plan_ref, bf16[128,1536]{1,0:T(8,128)(2,1)S(1)} %get-tuple-element.11.patch_ref, bf16[2,3,3,1536]{3,2,1,0:T(4,128)(2,1)S(1)} %get-tuple-element.12.modulation_ref, f32[12,128]{1,0:T(8,128)S(1)} %get-tuple-element.13.gain_ref, ...), custom_call_target="tpu_custom_call" | custom-call | flops 400000000 | bytes 8000000 | tf_op jit(solution)/shard_map/section_0_0/pallas_call | solution.py:223
  7.8 2.9 %collective-permute-start.1 = (bf16[776,128]{1,0:T(8,128)(2,1)S(1)}, bf16[776,128]{1,0:T(8,128)(2,1)S(1)}, u32[]{:S(2)}, u32[]{:S(2)}) collective-permute-start(bf16[776,128]{1,0:T(8,128)(2,1)S(1)} %section_0_0.1), channel_id=1, source_target_pairs={{0,2},{2,4},{4,6},{6,8},{8,10},{10,12},{12,14},{14,0},{1,3},{3,5},... | collective-permute-start | bytes 595976 | tf_op jit(solution)/shard_map/ppermute | solution.py:22
  10.7 1.8 %section_0_64.1 = bf16[776,128]{1,0:T(8,128)(2,1)S(1)} custom-call(s32[8]{0:T(128)S(4)} %get-tuple-element.10.plan_ref, bf16[128,1536]{1,0:T(8,128)(2,1)S(1)} %get-tuple-element.11.patch_ref, bf16[2,3,3,1536]{3,2,1,0:T(4,128)(2,1)S(1)} %get-tuple-element.12.modulation_ref, f32[12,128]{1,0:T(8,128)S(1)} %get-tuple-element.13.gain_ref, ...), custom_call_target="tpu_custom_call" | custom-call | flops 400000000 | bytes 8000000 | tf_op jit(solution)/shard_map/section_0_64/pallas_call | solution.py:223
  12.6 0.7 %collective-permute-start.3 = (bf16[776,128]{1,0:T(8,128)(2,1)S(1)}, bf16[776,128]{1,0:T(8,128)(2,1)S(1)}, u32[]{:S(2)}, u32[]{:S(2)}) collective-permute-start(bf16[776,128]{1,0:T(8,128)(2,1)S(1)} %section_0_64.1), channel_id=1, source_target_pairs={{0,2},{2,4},{4,6},{6,8},{8,10},{10,12},{12,14},{14,0},{1,3},{3,5},... | collective-permute-start | bytes 595976 | tf_op jit(solution)/shard_map/ppermute | solution.py:22
  13.3 5.1 %collective-permute-done.1.patch_ref = bf16[776,128]{1,0:T(8,128)(2,1)S(1)} collective-permute-done((bf16[776,128]{1,0:T(8,128)(2,1)S(1)}, bf16[776,128]{1,0:T(8,128)(2,1)S(1)}, u32[]{:S(2)}, u32[]{:S(2)}) %collective-permute-start.1) | collective-permute-done | bytes 198688 | tf_op jit(solution)/shard_map/ppermute | solution.py:22
  18.4 1.8 %section_1_0.1 = bf16[64,1536]{1,0:T(8,128)(2,1)S(1)} custom-call(s32[8]{0:T(128)S(4)} %get-tuple-element.10.plan_ref, bf16[776,128]{1,0:T(8,128)(2,1)S(1)} %collective-permute-done.1.patch_ref, bf16[2,3,3,1536]{3,2,1,0:T(4,128)(2,1)S(1)} %get-tuple-element.12.modulation_ref, f32[12,128]{1,0:T(8,128)S(1)} %get-tuple-element.13.gain_ref, ...), custom_call_target="tpu_custom_call" | custom-call | flops 400000000 | bytes 8000000 | tf_op jit(solution)/shard_map/section_1_0/pallas_call | solution.py:223
  20.3 0.2 collective-permute-start.2
  20.5 1.9 %collective-permute-done.3.patch_ref = bf16[776,128]{1,0:T(8,128)(2,1)S(1)} collective-permute-done((bf16[776,128]{1,0:T(8,128)(2,1)S(1)}, bf16[776,128]{1,0:T(8,128)(2,1)S(1)}, u32[]{:S(2)}, u32[]{:S(2)}) %collective-permute-start.3) | collective-permute-done | bytes 198688 | tf_op jit(solution)/shard_map/ppermute | solution.py:22
  22.4 1.8 %section_1_64.1 = bf16[64,1536]{1,0:T(8,128)(2,1)S(1)} custom-call(s32[8]{0:T(128)S(4)} %get-tuple-element.10.plan_ref, bf16[776,128]{1,0:T(8,128)(2,1)S(1)} %collective-permute-done.3.patch_ref, bf16[2,3,3,1536]{3,2,1,0:T(4,128)(2,1)S(1)} %get-tuple-element.12.modulation_ref, f32[12,128]{1,0:T(8,128)S(1)} %get-tuple-element.13.gain_ref, ...), custom_call_target="tpu_custom_call" | custom-call | flops 400000000 | bytes 8000000 | tf_op jit(solution)/shard_map/section_1_64/pallas_call | solution.py:223
  24.2 0.1 collective-permute-start.4
  24.3 5.0 %collective-permute-done.2 = bf16[64,1536]{1,0:T(8,128)(2,1)S(1)} collective-permute-done((bf16[64,1536]{1,0:T(8,128)(2,1)S(1)}, bf16[64,1536]{1,0:T(8,128)(2,1)S(1)}, u32[]{:S(2)}, u32[]{:S(2)}) %collective-permute-start.2) | collective-permute-done | bytes 196640 | tf_op jit(solution)/shard_map/ppermute | solution.py:22
  29.3 4.0 %collective-permute-done.4 = bf16[64,1536]{1,0:T(8,128)(2,1)S(1)} collective-permute-done((bf16[64,1536]{1,0:T(8,128)(2,1)S(1)}, bf16[64,1536]{1,0:T(8,128)(2,1)S(1)}, u32[]{:S(2)}, u32[]{:S(2)}) %collective-permute-start.4) | collective-permute-done | bytes 196640 | tf_op jit(solution)/shard_map/ppermute | solution.py:22
  33.3 0.8 %maximum_bitcast_fusion = bf16[1,128,1536]{2,1,0:T(8,128)(2,1)} fusion(bf16[64,1536]{1,0:T(8,128)(2,1)S(1)} %collective-permute-done.4, bf16[64,1536]{1,0:T(8,128)(2,1)S(1)} %collective-permute-done.2), kind=kLoop, calls=%fused_computation | loop fusion | flops 786432 | bytes 786432 | tf_op jit(solution)/shard_map/broadcast_in_dim | solution.py:259
Async XLA Ops:
  0.0 6.0 %collective-permute-start = (bf16[2,2,256,1536]{3,2,1,0:T(8,128)(2,1)}, bf16[2,2,256,1536]{3,2,1,0:T(8,128)(2,1)S(1)}, u32[]{:S(2)}, u32[]{:S(2)}) collective-permute-start(bf16[2,2,256,1536]{3,2,1,0:T(8,128)(2,1)} %bitcast.5), channel_id=1, source_target_pairs={{0,1},{1,0},{2,3},{3,2},{4,5},{5,4},{6,7},{7,6},{8,9},{9,8},{10,11... | collective-permute-start | bytes 9437192 | tf_op jit(solution)/shard_map/ppermute | solution.py:22
  7.8 10.6 %collective-permute-start.1 = (bf16[776,128]{1,0:T(8,128)(2,1)S(1)}, bf16[776,128]{1,0:T(8,128)(2,1)S(1)}, u32[]{:S(2)}, u32[]{:S(2)}) collective-permute-start(bf16[776,128]{1,0:T(8,128)(2,1)S(1)} %section_0_0.1), channel_id=1, source_target_pairs={{0,2},{2,4},{4,6},{6,8},{8,10},{10,12},{12,14},{14,0},{1,3},{3,5},... | collective-permute-start | bytes 595976 | tf_op jit(solution)/shard_map/ppermute | solution.py:22
  12.6 9.8 %collective-permute-start.3 = (bf16[776,128]{1,0:T(8,128)(2,1)S(1)}, bf16[776,128]{1,0:T(8,128)(2,1)S(1)}, u32[]{:S(2)}, u32[]{:S(2)}) collective-permute-start(bf16[776,128]{1,0:T(8,128)(2,1)S(1)} %section_0_64.1), channel_id=1, source_target_pairs={{0,2},{2,4},{4,6},{6,8},{8,10},{10,12},{12,14},{14,0},{1,3},{3,5},... | collective-permute-start | bytes 595976 | tf_op jit(solution)/shard_map/ppermute | solution.py:22
  20.3 9.0 %collective-permute-start.2 = (bf16[64,1536]{1,0:T(8,128)(2,1)S(1)}, bf16[64,1536]{1,0:T(8,128)(2,1)S(1)}, u32[]{:S(2)}, u32[]{:S(2)}) collective-permute-start(bf16[64,1536]{1,0:T(8,128)(2,1)S(1)} %section_1_0.1), channel_id=1, source_target_pairs={{0,2},{2,4},{4,6},{6,8},{8,10},{10,12},{12,14},{14,0},{1,3},{3,5},... | collective-permute-start | bytes 589832 | tf_op jit(solution)/shard_map/ppermute | solution.py:22
  24.2 9.1 %collective-permute-start.4 = (bf16[64,1536]{1,0:T(8,128)(2,1)S(1)}, bf16[64,1536]{1,0:T(8,128)(2,1)S(1)}, u32[]{:S(2)}, u32[]{:S(2)}) collective-permute-start(bf16[64,1536]{1,0:T(8,128)(2,1)S(1)} %section_1_64.1), channel_id=1, source_target_pairs={{0,2},{2,4},{4,6},{6,8},{8,10},{10,12},{12,14},{14,0},{1,3},{3,5},... | collective-permute-start | bytes 589832 | tf_op jit(solution)/shard_map/ppermute | solution.py:22

commit v3 on v2

--- a/solution.py
+++ b/solution.py
@@ -8,7 +8,8 @@
 from jax.sharding import PartitionSpec as P
 
 TICKS = 2
-CHUNKS = 2
+CHUNKS = 3
+UNIT = 16
 EPSILON = 1e-06
 EXTRA = 8
 
@@ -186,21 +187,37 @@
             (part * lax.rsqrt(power + EPSILON) * gain).astype(jnp.bfloat16)
             for part, power in zip(shifted, powers)
         ]
+        pairs = range(0, heads, 2)
+        doubles = [slice(head * head_dim, (head + 2) * head_dim) for head in pairs]
+        blank = jnp.zeros((rows, head_dim), jnp.bfloat16)
+        paired = [
+            jnp.concatenate(
+                [
+                    jnp.concatenate([queries[head], blank], axis=1),
+                    jnp.concatenate([blank, queries[head + 1]], axis=1),
+                ]
+            )
+            for head in pairs
+        ]
         scores = [
             lax.dot_general(
                 query, tiles(0, cols), (((1,), (1,)), ((), ())), preferred_element_type=jnp.float32
             )
-            for query, cols in zip(queries, blocks)
+            for query, cols in zip(paired, doubles)
         ]
         tops = [jnp.max(part, axis=-1, keepdims=True) for part in scores]
         weights = [jnp.exp2((part - top) * scale) for part, top in zip(scores, tops)]
         totals = [jnp.sum(part, axis=-1, keepdims=True) for part in weights]
         blended = [
             jnp.dot(part.astype(jnp.bfloat16), tiles(1, cols), preferred_element_type=jnp.float32)
-            for part, cols in zip(weights, blocks)
-        ]
-        for part, blend, total, cols in zip(state, blended, totals, blocks):
-            state_ref[:, cols] = part + mods[2:3, cols] * (blend / total)
+            for part, cols in zip(weights, doubles)
+        ]
+        for head, blend, total in zip(pairs, blended, totals):
+            for side in range(2):
+                cols = blocks[head + side]
+                span = slice(side * rows, (side + 1) * rows)
+                share = blend[span, side * head_dim : (side + 1) * head_dim] / total[span]
+                state_ref[:, cols] = state[head + side] + mods[2:3, cols] * share
 
     layer(0)
     for slot in range(1, slots):
@@ -232,6 +249,34 @@
     )(plan, pinned(patch), pinned(modulation), pinned(gains), pinned(own), pinned(other))
 
 
+def place_kernel(starts, *refs):
+    pieces, out_ref, sems = refs[: len(starts)], refs[-2], refs[-1]
+    copies = [
+        pltpu.make_async_copy(piece, out_ref.at[pl.ds(start, piece.shape[0])], sems.at[i])
+        for i, (start, piece) in enumerate(zip(starts, pieces))
+    ]
+    for copy in copies:
+        copy.start()
+    for copy in copies:
+        copy.wait()
+
+
+def place(starts, pieces, tokens, into=None):
+    width = pieces[0].shape[1]
+    extra = [] if into is None else [pinned(into, pltpu.HBM)]
+    return pl.pallas_call(
+        functools.partial(place_kernel, starts),
+        out_shape=pltpu.HBM((tokens, width), pieces[0].dtype),
+        in_specs=[VMEM] * len(pieces) + [ANY] * len(extra),
+        out_specs=ANY,
+        scratch_shapes=[pltpu.SemaphoreType.DMA((len(pieces),))],
+        input_output_aliases={} if into is None else {len(pieces): 0},
+        compiler_params=pltpu.CompilerParams(vmem_limit_bytes=4 << 20),
+        cost_estimate=pl.CostEstimate(flops=0, bytes_accessed=600_000, transcendentals=0),
+        name=f"place_{starts[0]}",
+    )(*(pinned(piece) for piece in pieces), *extra)
+
+
 def per_device(
     patches, positions, timesteps, section_bounds, tile_neighbours, modulation, query_gain, stale_kv
 ):
@@ -243,20 +288,23 @@
     plan, patch, mods, gains, own = stage(
         section_bounds, tile_neighbours.T, positions, timesteps, patches[0], modulation, query_gain, own_hbm
     )
-    rows = tokens // CHUNKS
+    units = tokens // UNIT
+    sizes = [UNIT * ((units + CHUNKS - 1 - chunk) // CHUNKS) for chunk in range(CHUNKS)]
+    starts = [sum(sizes[:chunk]) for chunk in range(CHUNKS)]
     pieces = [patch] * CHUNKS
     for tick in range(TICKS):
         pieces = [
             from_behind(
                 run_section(
-                    tick, chunk * rows, rows, cycle_size, pipe, width, plan, piece, mods, gains, own, other
+                    tick, starts[chunk], sizes[chunk], cycle_size, pipe, width, plan, piece, mods, gains, own, other
                 ),
                 "segment",
                 1,
             )
             for chunk, piece in enumerate(pieces)
         ]
-    return jnp.concatenate(pieces)[None]
+    placed = place(starts[:-1], pieces[:-1], tokens)
+    return place(starts[-1:], pieces[-1:], tokens, placed)[None]
 
 
 def solution(mesh):

time: 34.2 us -> 32.4 us (0.947)
  waiting for transfers between devices: 18.1 us -> 9.57 us
  starting transfers between devices: 4.32 us -> 12.7 us
  other arithmetic: 0.77 us -> 0 us
  Pallas kernels: 9.48 us -> 8.73 us
    ppermute x5 -> x7, waiting for transfers between devices: 18.1 us -> 9.57 us  [from_behind(): lax.ppermute(x, axis, [(i, (i + by) % devices) for i in range(devices)])]
    ppermute x5 -> x7, starting transfers between devices: 4.32 us -> 12.7 us  [from_behind(): lax.ppermute(x, axis, [(i, (i + by) % devices) for i in range(devices)])]
    pallas_call x4 -> x6, Pallas kernels: 7.37 us -> 5.25 us  [run_section(): pl.pallas_call(functools.partial(section_kernel, tick, start, cycle_size,...]
    pallas_call x0 -> x2, Pallas kernels: none -> 1.37 us  [place(): pl.pallas_call(functools.partial(place_kernel, starts), out_shape=pltpu.H...]
    broadcast_in_dim x1 -> x0, other arithmetic: 0.77 us -> none  [per_device(): return jnp.concatenate(pieces)[None]]
  transfers between devices with their start and end apart: 5 -> 7, of which waited for: 5 -> 6; matrix products, arithmetic and copies ran while one was open for 0% -> 0% of each run, Pallas kernels for 22% -> 22%
where the time goes in v3:
time: 32.4 us; the launch traced here: 32.3 us
  starting transfers between devices  12.7 us (39%)
  waiting for transfers between devices  9.57 us (30%)
  Pallas kernels  8.73 us (27%)
  between operations  1.37 us (4%)
    ppermute x7, starting transfers between devices, from_behind(): lax.ppermute(x, axis, [(i, (i + by) % devices) for i in range(devices)])  12.7 us
    ppermute x7, waiting for transfers between devices, from_behind(): lax.ppermute(x, axis, [(i, (i + by) % devices) for i in range(devices)])  9.57 us
    pallas_call x6, Pallas kernels, run_section(): pl.pallas_call(functools.partial(section_kernel, tick, start, cycle_size,...  5.25 us
    pallas_call x1, Pallas kernels, stage(): pl.pallas_call(stage_kernel, out_shape=(pltpu.SMEM((plan_size,), jnp.int3...  2.11 us
    pallas_call x2, Pallas kernels, place(): pl.pallas_call(functools.partial(place_kernel, starts), out_shape=pltpu.H...  1.37 us
  transfers between devices with their start and end apart: 7, of which 6 were waited for; matrix products, arithmetic and copies ran while one was open for 0% of the time, Pallas kernels for 22%

profile of v3, /device:TPU:0, one launch (start us, length us, event | category | flops | bytes accessed | tf_op | source)
XLA Modules:
  0.0 32.3 jit_solution(17346744164376788645)
XLA Ops:
  0.0 0.5 %collective-permute-start = (bf16[2,2,256,1536]{3,2,1,0:T(8,128)(2,1)}, bf16[2,2,256,1536]{3,2,1,0:T(8,128)(2,1)S(1)}, u32[]{:S(2)}, u32[]{:S(2)}) collective-permute-start(bf16[2,2,256,1536]{3,2,1,0:T(8,128)(2,1)} %bitcast.4), channel_id=1, source_target_pairs={{0,1},{1,0},{2,3},{3,2},{4,5},{5,4},{6,7},{7,6},{8,9},{9,8},{10,11... | collective-permute-start | bytes 9437192 | tf_op jit(solution)/shard_map/ppermute | solution.py:23
  1.8 2.1 %stage.1 = (s32[8]{0:T(128)S(4)}, bf16[128,1536]{1,0:T(8,128)(2,1)S(1)}, bf16[2,3,3,1536]{3,2,1,0:T(4,128)(2,1)S(1)}, f32[12,128]{1,0:T(8,128)S(1)}, bf16[2,2,256,1536]{3,2,1,0:T(8,128)(2,1)S(1)}) custom-call(s32[9]{0:T(128)} %bounds_hbm.1, s32[2,4]{1,0:T(2,128)} %bitcast.7, s32[1]{0:T(128)S(6)} %copy.11.position_ref, s32[1]{0:T(128)S(6)} %copy.12.step_ref, ...), custom_call_target="tpu_custom_call" | custom-call | bytes 7000000 | tf_op jit(solution)/shard_map/stage/pallas_call | solution.py:93
  3.9 2.1 %collective-permute-done.other_ref = bf16[2,2,256,1536]{3,2,1,0:T(8,128)(2,1)S(1)} collective-permute-done((bf16[2,2,256,1536]{3,2,1,0:T(8,128)(2,1)}, bf16[2,2,256,1536]{3,2,1,0:T(8,128)(2,1)S(1)}, u32[]{:S(2)}, u32[]{:S(2)}) %collective-permute-start) | collective-permute-done | bytes 3145760 | tf_op jit(solution)/shard_map/ppermute | solution.py:23
  6.0 0.9 %section_0_0.1 = bf16[584,128]{1,0:T(8,128)(2,1)S(1)} custom-call(s32[8]{0:T(128)S(4)} %get-tuple-element.10.plan_ref, bf16[128,1536]{1,0:T(8,128)(2,1)S(1)} %get-tuple-element.11.patch_ref, bf16[2,3,3,1536]{3,2,1,0:T(4,128)(2,1)S(1)} %get-tuple-element.12.modulation_ref, f32[12,128]{1,0:T(8,128)S(1)} %get-tuple-element.13.gain_ref, ...), custom_call_target="tpu_custom_call" | custom-call | flops 400000000 | bytes 8000000 | tf_op jit(solution)/shard_map/section_0_0/pallas_call | solution.py:240
  6.9 2.9 %collective-permute-start.3 = (bf16[584,128]{1,0:T(8,128)(2,1)S(1)}, bf16[584,128]{1,0:T(8,128)(2,1)S(1)}, u32[]{:S(2)}, u32[]{:S(2)}) collective-permute-start(bf16[584,128]{1,0:T(8,128)(2,1)S(1)} %section_0_0.1), channel_id=1, source_target_pairs={{0,2},{2,4},{4,6},{6,8},{8,10},{10,12},{12,14},{14,0},{1,3},{3,5},... | collective-permute-start | bytes 448520 | tf_op jit(solution)/shard_map/ppermute | solution.py:23
  9.8 0.9 %section_0_48.1 = bf16[584,128]{1,0:T(8,128)(2,1)S(1)} custom-call(s32[8]{0:T(128)S(4)} %get-tuple-element.10.plan_ref, bf16[128,1536]{1,0:T(8,128)(2,1)S(1)} %get-tuple-element.11.patch_ref, bf16[2,3,3,1536]{3,2,1,0:T(4,128)(2,1)S(1)} %get-tuple-element.12.modulation_ref, f32[12,128]{1,0:T(8,128)S(1)} %get-tuple-element.13.gain_ref, ...), custom_call_target="tpu_custom_call" | custom-call | flops 400000000 | bytes 8000000 | tf_op jit(solution)/shard_map/section_0_48/pallas_call | solution.py:240
  10.7 2.5 %collective-permute-start.5 = (bf16[584,128]{1,0:T(8,128)(2,1)S(1)}, bf16[584,128]{1,0:T(8,128)(2,1)S(1)}, u32[]{:S(2)}, u32[]{:S(2)}) collective-permute-start(bf16[584,128]{1,0:T(8,128)(2,1)S(1)} %section_0_48.1), channel_id=1, source_target_pairs={{0,2},{2,4},{4,6},{6,8},{8,10},{10,12},{12,14},{14,0},{1,3},{3,5},... | collective-permute-start | bytes 448520 | tf_op jit(solution)/shard_map/ppermute | solution.py:23
  13.2 0.8 %section_0_96.1 = bf16[392,128]{1,0:T(8,128)(2,1)S(1)} custom-call(s32[8]{0:T(128)S(4)} %get-tuple-element.10.plan_ref, bf16[128,1536]{1,0:T(8,128)(2,1)S(1)} %get-tuple-element.11.patch_ref, bf16[2,3,3,1536]{3,2,1,0:T(4,128)(2,1)S(1)} %get-tuple-element.12.modulation_ref, f32[12,128]{1,0:T(8,128)S(1)} %get-tuple-element.13.gain_ref, ...), custom_call_target="tpu_custom_call" | custom-call | flops 400000000 | bytes 8000000 | tf_op jit(solution)/shard_map/section_0_96/pallas_call | solution.py:240
  14.0 2.4 %collective-permute-start.1 = (bf16[392,128]{1,0:T(8,128)(2,1)S(1)}, bf16[392,128]{1,0:T(8,128)(2,1)S(1)}, u32[]{:S(2)}, u32[]{:S(2)}) collective-permute-start(bf16[392,128]{1,0:T(8,128)(2,1)S(1)} %section_0_96.1), channel_id=1, source_target_pairs={{0,2},{2,4},{4,6},{6,8},{8,10},{10,12},{12,14},{14,0},{1,3},{3,5},... | collective-permute-start | bytes 301064 | tf_op jit(solution)/shard_map/ppermute | solution.py:23
  16.5 1.1 %collective-permute-done.3.patch_ref = bf16[584,128]{1,0:T(8,128)(2,1)S(1)} collective-permute-done((bf16[584,128]{1,0:T(8,128)(2,1)S(1)}, bf16[584,128]{1,0:T(8,128)(2,1)S(1)}, u32[]{:S(2)}, u32[]{:S(2)}) %collective-permute-start.3) | collective-permute-done | bytes 149536 | tf_op jit(solution)/shard_map/ppermute | solution.py:23
  17.6 0.9 %section_1_0.1 = bf16[48,1536]{1,0:T(8,128)(2,1)S(1)} custom-call(s32[8]{0:T(128)S(4)} %get-tuple-element.10.plan_ref, bf16[584,128]{1,0:T(8,128)(2,1)S(1)} %collective-permute-done.3.patch_ref, bf16[2,3,3,1536]{3,2,1,0:T(4,128)(2,1)S(1)} %get-tuple-element.12.modulation_ref, f32[12,128]{1,0:T(8,128)S(1)} %get-tuple-element.13.gain_ref, ...), custom_call_target="tpu_custom_call" | custom-call | flops 400000000 | bytes 8000000 | tf_op jit(solution)/shard_map/section_1_0/pallas_call | solution.py:240
  18.5 1.3 %collective-permute-start.4 = (bf16[48,1536]{1,0:T(8,128)(2,1)S(1)}, bf16[48,1536]{1,0:T(8,128)(2,1)S(1)}, u32[]{:S(2)}, u32[]{:S(2)}) collective-permute-start(bf16[48,1536]{1,0:T(8,128)(2,1)S(1)} %section_1_0.1), channel_id=1, source_target_pairs={{0,2},{2,4},{4,6},{6,8},{8,10},{10,12},{12,14},{14,0},{1,3},{3,5},... | collective-permute-start | bytes 442376 | tf_op jit(solution)/shard_map/ppermute | solution.py:23
  19.8 1.0 %collective-permute-done.5.patch_ref = bf16[584,128]{1,0:T(8,128)(2,1)S(1)} collective-permute-done((bf16[584,128]{1,0:T(8,128)(2,1)S(1)}, bf16[584,128]{1,0:T(8,128)(2,1)S(1)}, u32[]{:S(2)}, u32[]{:S(2)}) %collective-permute-start.5) | collective-permute-done | bytes 149536 | tf_op jit(solution)/shard_map/ppermute | solution.py:23
  20.8 0.9 %section_1_48.1 = bf16[48,1536]{1,0:T(8,128)(2,1)S(1)} custom-call(s32[8]{0:T(128)S(4)} %get-tuple-element.10.plan_ref, bf16[584,128]{1,0:T(8,128)(2,1)S(1)} %collective-permute-done.5.patch_ref, bf16[2,3,3,1536]{3,2,1,0:T(4,128)(2,1)S(1)} %get-tuple-element.12.modulation_ref, f32[12,128]{1,0:T(8,128)S(1)} %get-tuple-element.13.gain_ref, ...), custom_call_target="tpu_custom_call" | custom-call | flops 400000000 | bytes 8000000 | tf_op jit(solution)/shard_map/section_1_48/pallas_call | solution.py:240
  21.7 1.4 %collective-permute-start.6 = (bf16[48,1536]{1,0:T(8,128)(2,1)S(1)}, bf16[48,1536]{1,0:T(8,128)(2,1)S(1)}, u32[]{:S(2)}, u32[]{:S(2)}) collective-permute-start(bf16[48,1536]{1,0:T(8,128)(2,1)S(1)} %section_1_48.1), channel_id=1, source_target_pairs={{0,2},{2,4},{4,6},{6,8},{8,10},{10,12},{12,14},{14,0},{1,3},{3,5},... | collective-permute-start | bytes 442376 | tf_op jit(solution)/shard_map/ppermute | solution.py:23
  23.1 0.0 collective-permute-done.1.patch_ref
  23.1 0.8 %section_1_96.1 = bf16[32,1536]{1,0:T(8,128)(2,1)S(1)} custom-call(s32[8]{0:T(128)S(4)} %get-tuple-element.10.plan_ref, bf16[392,128]{1,0:T(8,128)(2,1)S(1)} %collective-permute-done.1.patch_ref, bf16[2,3,3,1536]{3,2,1,0:T(4,128)(2,1)S(1)} %get-tuple-element.12.modulation_ref, f32[12,128]{1,0:T(8,128)S(1)} %get-tuple-element.13.gain_ref, ...), custom_call_target="tpu_custom_call" | custom-call | flops 400000000 | bytes 8000000 | tf_op jit(solution)/shard_map/section_1_96/pallas_call | solution.py:240
  24.0 1.6 %collective-permute-start.2 = (bf16[32,1536]{1,0:T(8,128)(2,1)S(1)}, bf16[32,1536]{1,0:T(8,128)(2,1)S(1)}, u32[]{:S(2)}, u32[]{:S(2)}) collective-permute-start(bf16[32,1536]{1,0:T(8,128)(2,1)S(1)} %section_1_96.1), channel_id=1, source_target_pairs={{0,2},{2,4},{4,6},{6,8},{8,10},{10,12},{12,14},{14,0},{1,3},{3,5},... | collective-permute-start | bytes 294920 | tf_op jit(solution)/shard_map/ppermute | solution.py:23
  25.6 1.1 %collective-permute-done.4.refs_0_ = bf16[48,1536]{1,0:T(8,128)(2,1)S(1)} collective-permute-done((bf16[48,1536]{1,0:T(8,128)(2,1)S(1)}, bf16[48,1536]{1,0:T(8,128)(2,1)S(1)}, u32[]{:S(2)}, u32[]{:S(2)}) %collective-permute-start.4) | collective-permute-done | bytes 147488 | tf_op jit(solution)/shard_map/ppermute | solution.py:23
  26.7 3.9 %collective-permute-done.6.refs_1_ = bf16[48,1536]{1,0:T(8,128)(2,1)S(1)} collective-permute-done((bf16[48,1536]{1,0:T(8,128)(2,1)S(1)}, bf16[48,1536]{1,0:T(8,128)(2,1)S(1)}, u32[]{:S(2)}, u32[]{:S(2)}) %collective-permute-start.6) | collective-permute-done | bytes 147488 | tf_op jit(solution)/shard_map/ppermute | solution.py:23
  30.6 0.7 %place_0.1.refs_1_ = bf16[128,1536]{1,0:T(8,128)(2,1)} custom-call(bf16[48,1536]{1,0:T(8,128)(2,1)S(1)} %collective-permute-done.4.refs_0_, bf16[48,1536]{1,0:T(8,128)(2,1)S(1)} %collective-permute-done.6.refs_1_), custom_call_target="tpu_custom_call" | custom-call | bytes 600000 | tf_op jit(solution)/shard_map/place_0/pallas_call | solution.py:267
  31.4 0.3 collective-permute-done.2.refs_0_
  31.7 0.6 %place_96.1 = bf16[128,1536]{1,0:T(8,128)(2,1)} custom-call(bf16[32,1536]{1,0:T(8,128)(2,1)S(1)} %collective-permute-done.2.refs_0_, bf16[128,1536]{1,0:T(8,128)(2,1)} %place_0.1.refs_1_), custom_call_target="tpu_custom_call", output_to_operand_aliasing={{}: (1, {})} | custom-call | bytes 600000 | tf_op jit(solution)/shard_map/place_96/pallas_call | solution.py:267
Async XLA Ops:
  0.0 6.0 %collective-permute-start = (bf16[2,2,256,1536]{3,2,1,0:T(8,128)(2,1)}, bf16[2,2,256,1536]{3,2,1,0:T(8,128)(2,1)S(1)}, u32[]{:S(2)}, u32[]{:S(2)}) collective-permute-start(bf16[2,2,256,1536]{3,2,1,0:T(8,128)(2,1)} %bitcast.4), channel_id=1, source_target_pairs={{0,1},{1,0},{2,3},{3,2},{4,5},{5,4},{6,7},{7,6},{8,9},{9,8},{10,11... | collective-permute-start | bytes 9437192 | tf_op jit(solution)/shard_map/ppermute | solution.py:23
  6.9 10.7 %collective-permute-start.3 = (bf16[584,128]{1,0:T(8,128)(2,1)S(1)}, bf16[584,128]{1,0:T(8,128)(2,1)S(1)}, u32[]{:S(2)}, u32[]{:S(2)}) collective-permute-start(bf16[584,128]{1,0:T(8,128)(2,1)S(1)} %section_0_0.1), channel_id=1, source_target_pairs={{0,2},{2,4},{4,6},{6,8},{8,10},{10,12},{12,14},{14,0},{1,3},{3,5},... | collective-permute-start | bytes 448520 | tf_op jit(solution)/shard_map/ppermute | solution.py:23
  10.7 10.1 %collective-permute-start.5 = (bf16[584,128]{1,0:T(8,128)(2,1)S(1)}, bf16[584,128]{1,0:T(8,128)(2,1)S(1)}, u32[]{:S(2)}, u32[]{:S(2)}) collective-permute-start(bf16[584,128]{1,0:T(8,128)(2,1)S(1)} %section_0_48.1), channel_id=1, source_target_pairs={{0,2},{2,4},{4,6},{6,8},{8,10},{10,12},{12,14},{14,0},{1,3},{3,5},... | collective-permute-start | bytes 448520 | tf_op jit(solution)/shard_map/ppermute | solution.py:23
  14.0 9.1 %collective-permute-start.1 = (bf16[392,128]{1,0:T(8,128)(2,1)S(1)}, bf16[392,128]{1,0:T(8,128)(2,1)S(1)}, u32[]{:S(2)}, u32[]{:S(2)}) collective-permute-start(bf16[392,128]{1,0:T(8,128)(2,1)S(1)} %section_0_96.1), channel_id=1, source_target_pairs={{0,2},{2,4},{4,6},{6,8},{8,10},{10,12},{12,14},{14,0},{1,3},{3,5},... | collective-permute-start | bytes 301064 | tf_op jit(solution)/shard_map/ppermute | solution.py:23
  18.5 8.2 %collective-permute-start.4 = (bf16[48,1536]{1,0:T(8,128)(2,1)S(1)}, bf16[48,1536]{1,0:T(8,128)(2,1)S(1)}, u32[]{:S(2)}, u32[]{:S(2)}) collective-permute-start(bf16[48,1536]{1,0:T(8,128)(2,1)S(1)} %section_1_0.1), channel_id=1, source_target_pairs={{0,2},{2,4},{4,6},{6,8},{8,10},{10,12},{12,14},{14,0},{1,3},{3,5},... | collective-permute-start | bytes 442376 | tf_op jit(solution)/shard_map/ppermute | solution.py:23
  21.7 8.9 %collective-permute-start.6 = (bf16[48,1536]{1,0:T(8,128)(2,1)S(1)}, bf16[48,1536]{1,0:T(8,128)(2,1)S(1)}, u32[]{:S(2)}, u32[]{:S(2)}) collective-permute-start(bf16[48,1536]{1,0:T(8,128)(2,1)S(1)} %section_1_48.1), channel_id=1, source_target_pairs={{0,2},{2,4},{4,6},{6,8},{8,10},{10,12},{12,14},{14,0},{1,3},{3,5},... | collective-permute-start | bytes 442376 | tf_op jit(solution)/shard_map/ppermute | solution.py:23
  24.0 7.7 %collective-permute-start.2 = (bf16[32,1536]{1,0:T(8,128)(2,1)S(1)}, bf16[32,1536]{1,0:T(8,128)(2,1)S(1)}, u32[]{:S(2)}, u32[]{:S(2)}) collective-permute-start(bf16[32,1536]{1,0:T(8,128)(2,1)S(1)} %section_1_96.1), channel_id=1, source_target_pairs={{0,2},{2,4},{4,6},{6,8},{8,10},{10,12},{12,14},{14,0},{1,3},{3,5},... | collective-permute-start | bytes 294920 | tf_op jit(solution)/shard_map/ppermute | solution.py:23

commit v4 on v3

--- a/solution.py
+++ b/solution.py
@@ -25,6 +25,40 @@
 
 def pinned(x, space=pltpu.VMEM):
     return pltpu.with_memory_space_constraint(x, space)
+
+
+def head_blocks(width, head_dim):
+    return [slice(start, start + head_dim) for start in range(0, width, head_dim)]
+
+
+def modulated_queries(state, mods, gain, blocks, width):
+    middle = jnp.sum(sum(state[1:], state[0]), axis=-1, keepdims=True) / width
+    centred = [part - middle for part in state]
+    squares = [part * part for part in centred]
+    spread = jnp.sum(sum(squares[1:], squares[0]), axis=-1, keepdims=True) / width
+    sharp = lax.rsqrt(spread + EPSILON)
+    shifted = [part * sharp * (1.0 + mods[1:2, cols]) + mods[0:1, cols] for part, cols in zip(centred, blocks)]
+    powers = [jnp.mean(part * part, axis=-1, keepdims=True) for part in shifted]
+    return [
+        (part * lax.rsqrt(power + EPSILON) * gain).astype(jnp.bfloat16) for part, power in zip(shifted, powers)
+    ]
+
+
+def paired_queries(queries):
+    blank = jnp.zeros_like(queries[0])
+    return [
+        jnp.concatenate(
+            [
+                jnp.concatenate([queries[head], blank], axis=1),
+                jnp.concatenate([blank, queries[head + 1]], axis=1),
+            ]
+        )
+        for head in range(0, len(queries), 2)
+    ]
+
+
+def transposed_dot(a, b):
+    return lax.dot_general(a, b, (((1,), (1,)), ((), ())), preferred_element_type=jnp.float32)
 
 
 def stage_kernel(
@@ -41,13 +75,18 @@
     modulation_out,
     gain_out,
     own_out,
+    query_out,
+    share_out,
+    top_out,
+    total_out,
     bounds_ref,
     neighbours_ref,
     sems,
 ):
     slots = own_ref.shape[0]
+    far = sems.shape[0] - slots
     small = [
-        pltpu.make_async_copy(source, target, sems.at[3 + slots + i])
+        pltpu.make_async_copy(source, target, sems.at[2 + slots + i])
         for i, (source, target) in enumerate(
             [
                 (bounds_hbm, bounds_ref),
@@ -58,9 +97,9 @@
     copies = [
         pltpu.make_async_copy(patch_ref, patch_out, sems.at[0]),
         pltpu.make_async_copy(gain_ref, gain_out, sems.at[1]),
-        pltpu.make_async_copy(own_ref, own_out, sems.at[2]),
-    ]
-    for copy in small + copies:
+    ]
+    slabs = [pltpu.make_async_copy(own_ref.at[slot], own_out.at[slot], sems.at[far + slot]) for slot in range(slots)]
+    for copy in small + copies + slabs:
         copy.start()
     for copy in small:
         copy.wait()
@@ -72,7 +111,7 @@
     first_layer = bounds_ref[section]
     for slot in range(slots):
         layer_now = jnp.minimum(first_layer + slot, layers - 1)
-        copy = pltpu.make_async_copy(modulation_ref.at[:, layer_now], modulation_out.at[slot], sems.at[3 + slot])
+        copy = pltpu.make_async_copy(modulation_ref.at[:, layer_now], modulation_out.at[slot], sems.at[2 + slot])
         copy.start()
         copies.append(copy)
     slab = neighbours_ref.shape[1] // 2
@@ -85,6 +124,39 @@
         plan_ref[4 + slab + place] = lax.rem(neighbours_ref[1, space * slab + place], slab)
     for copy in copies:
         copy.wait()
+    slabs[0].wait()
+
+    tile = own_ref.shape[2] // slab
+    rows, width = patch_ref.shape
+    head_dim = gain_ref.shape[1]
+    blocks = head_blocks(width, head_dim)
+    own_row = pl.multiple_of(plan_ref[4 + position_ref[0]] * tile, tile)
+    scale = head_dim ** -0.5 * math.log2(math.e)
+    mods = modulation_out[0, step_ref[0]].astype(jnp.float32)
+    gain = gain_out[pl.ds(first_layer, 1), :]
+    state = [patch_out[:, cols].astype(jnp.float32) for cols in blocks]
+    queries = modulated_queries(state, mods, gain, blocks, width)
+    scores = [
+        transposed_dot(query, own_out[0, 0, pl.ds(own_row, tile), cols]) for query, cols in zip(queries, blocks)
+    ]
+    tops = [jnp.max(part, axis=-1, keepdims=True) for part in scores]
+    weights = [jnp.exp2((part - top) * scale) for part, top in zip(scores, tops)]
+    totals = [jnp.sum(part, axis=-1, keepdims=True) for part in weights]
+    shares = [
+        jnp.dot(
+            part.astype(jnp.bfloat16),
+            own_out[0, 1, pl.ds(own_row, tile), cols],
+            preferred_element_type=jnp.float32,
+        )
+        for part, cols in zip(weights, blocks)
+    ]
+    for head, cols in enumerate(blocks):
+        query_out[:, cols] = queries[head]
+        share_out[:, cols] = shares[head]
+        top_out[:, cols] = jnp.broadcast_to(tops[head], shares[head].shape)
+        total_out[:, cols] = jnp.broadcast_to(totals[head], shares[head].shape)
+    for copy in slabs[1:]:
+        copy.wait()
 
 
 def stage(bounds, neighbours, position, step, patch, modulation, gains, own):
@@ -98,13 +170,17 @@
             pltpu.VMEM((slots, modulation.shape[0]) + modulation.shape[2:], modulation.dtype),
             pltpu.VMEM(gains.shape, gains.dtype),
             pltpu.VMEM(own.shape, own.dtype),
+            pltpu.VMEM(patch.shape, jnp.bfloat16),
+            pltpu.VMEM(patch.shape, jnp.float32),
+            pltpu.VMEM(patch.shape, jnp.float32),
+            pltpu.VMEM(patch.shape, jnp.float32),
         ),
         in_specs=[ANY] * 2 + [SMEM] * 2 + [ANY] * 4,
-        out_specs=(SMEM, VMEM, VMEM, VMEM, VMEM),
+        out_specs=(SMEM,) + (VMEM,) * 8,
         scratch_shapes=[pltpu.SMEM(x.shape, x.dtype) for x in (bounds, neighbours)]
-        + [pltpu.SemaphoreType.DMA((5 + slots,))],
+        + [pltpu.SemaphoreType.DMA((4 + 2 * slots,))],
         compiler_params=pltpu.CompilerParams(vmem_limit_bytes=16 << 20),
-        cost_estimate=pl.CostEstimate(flops=0, bytes_accessed=7_000_000, transcendentals=0),
+        cost_estimate=pl.CostEstimate(flops=100_000_000, bytes_accessed=8_000_000, transcendentals=200_000),
         name="stage",
     )(
         pinned(bounds, pltpu.HBM),
@@ -126,9 +202,9 @@
     gain_ref,
     own_ref,
     other_ref,
-    out_ref,
-    state_ref,
+    *refs,
 ):
+    half, (out_ref, state_ref) = refs[:-2], refs[-2:]
     rows, width = state_ref.shape
     layers, head_dim = gain_ref.shape
     heads = width // head_dim
@@ -163,61 +239,52 @@
         layer_now = jnp.minimum(first_layer + slot, layers - 1)
         mods = modulation_ref[slot, row].astype(jnp.float32)
         gain = gain_ref[pl.ds(layer_now, 1), :]
-        blocks = [slice(head * head_dim, (head + 1) * head_dim) for head in range(heads)]
+        blocks = head_blocks(width, head_dim)
+        pairs = range(0, heads, 2)
+        doubles = head_blocks(width, 2 * head_dim)
+        split = tick == 0 and slot == 0
 
         def tiles(kind, cols):
-            return jnp.concatenate(
-                [
-                    own_ref[slot, kind, pl.ds(own_row, tile), cols],
-                    other_ref[slot, kind, pl.ds(other_row, tile), cols],
-                ]
-            )
+            theirs = other_ref[slot, kind, pl.ds(other_row, tile), cols]
+            if split:
+                return theirs
+            return jnp.concatenate([own_ref[slot, kind, pl.ds(own_row, tile), cols], theirs])
 
         state = [state_ref[:, cols] for cols in blocks]
-        middle = jnp.sum(sum(state[1:], state[0]), axis=-1, keepdims=True) / width
-        centred = [part - middle for part in state]
-        squares = [part * part for part in centred]
-        spread = jnp.sum(sum(squares[1:], squares[0]), axis=-1, keepdims=True) / width
-        sharp = lax.rsqrt(spread + EPSILON)
-        shifted = [
-            part * sharp * (1.0 + mods[1:2, cols]) + mods[0:1, cols] for part, cols in zip(centred, blocks)
-        ]
-        powers = [jnp.mean(part * part, axis=-1, keepdims=True) for part in shifted]
-        queries = [
-            (part * lax.rsqrt(power + EPSILON) * gain).astype(jnp.bfloat16)
-            for part, power in zip(shifted, powers)
-        ]
-        pairs = range(0, heads, 2)
-        doubles = [slice(head * head_dim, (head + 2) * head_dim) for head in pairs]
-        blank = jnp.zeros((rows, head_dim), jnp.bfloat16)
-        paired = [
-            jnp.concatenate(
-                [
-                    jnp.concatenate([queries[head], blank], axis=1),
-                    jnp.concatenate([blank, queries[head + 1]], axis=1),
-                ]
-            )
-            for head in pairs
-        ]
-        scores = [
-            lax.dot_general(
-                query, tiles(0, cols), (((1,), (1,)), ((), ())), preferred_element_type=jnp.float32
-            )
-            for query, cols in zip(paired, doubles)
-        ]
+        if split:
+            query_ref, share_ref, top_ref, total_ref = half
+            window = slice(start, start + rows)
+            queries = [query_ref[window, cols] for cols in blocks]
+        else:
+            queries = modulated_queries(state, mods, gain, blocks, width)
+        paired = paired_queries(queries)
+        scores = [transposed_dot(query, tiles(0, cols)) for query, cols in zip(paired, doubles)]
         tops = [jnp.max(part, axis=-1, keepdims=True) for part in scores]
+        if split:
+            own_tops = [
+                jnp.concatenate([top_ref[window, blocks[head]], top_ref[window, blocks[head + 1]]])
+                for head in pairs
+            ]
+            tops = [jnp.maximum(top, own_top) for top, own_top in zip(tops, own_tops)]
+            fades = [jnp.exp2((own_top - top) * scale) for top, own_top in zip(tops, own_tops)]
         weights = [jnp.exp2((part - top) * scale) for part, top in zip(scores, tops)]
         totals = [jnp.sum(part, axis=-1, keepdims=True) for part in weights]
         blended = [
             jnp.dot(part.astype(jnp.bfloat16), tiles(1, cols), preferred_element_type=jnp.float32)
             for part, cols in zip(weights, doubles)
         ]
-        for head, blend, total in zip(pairs, blended, totals):
+        for pair, (blend, total) in enumerate(zip(blended, totals)):
             for side in range(2):
-                cols = blocks[head + side]
+                head = 2 * pair + side
+                cols = blocks[head]
                 span = slice(side * rows, (side + 1) * rows)
-                share = blend[span, side * head_dim : (side + 1) * head_dim] / total[span]
-                state_ref[:, cols] = state[head + side] + mods[2:3, cols] * share
+                share = blend[span, side * head_dim : (side + 1) * head_dim]
+                whole = total[span]
+                if split:
+                    fade = fades[pair][span]
+                    share = share + fade * share_ref[window, cols]
+                    whole = whole + fade * total_ref[window, cols]
+                state_ref[:, cols] = state[head] + mods[2:3, cols] * (share / whole)
 
     layer(0)
     for slot in range(1, slots):
@@ -234,19 +301,19 @@
         out_ref[...] = state_ref[...].astype(out_ref.dtype)
 
 
-def run_section(tick, start, rows, cycle_size, pipe, width, plan, patch, modulation, gains, own, other):
+def run_section(tick, start, rows, cycle_size, pipe, width, plan, patch, modulation, gains, own, other, half):
     heads = width // gains.shape[1]
     shape = (heads * rows + EXTRA, gains.shape[1]) if tick == 0 else (rows, width)
     return pl.pallas_call(
         functools.partial(section_kernel, tick, start, cycle_size, pipe),
         out_shape=pltpu.VMEM(shape, jnp.bfloat16),
-        in_specs=[SMEM] + [VMEM] * 5,
+        in_specs=[SMEM] + [VMEM] * (5 + len(half)),
         out_specs=VMEM,
         scratch_shapes=[pltpu.VMEM((rows, width), jnp.float32)],
         compiler_params=pltpu.CompilerParams(vmem_limit_bytes=16 << 20),
         cost_estimate=pl.CostEstimate(flops=400_000_000, bytes_accessed=8_000_000, transcendentals=800_000),
         name=f"section_{tick}_{start}",
-    )(plan, pinned(patch), pinned(modulation), pinned(gains), pinned(own), pinned(other))
+    )(plan, pinned(patch), pinned(modulation), pinned(gains), pinned(own), pinned(other), *(pinned(x) for x in half))
 
 
 def place_kernel(starts, *refs):
@@ -285,7 +352,7 @@
     cycle_size = lax.axis_size("segment")
     pipe = section_bounds.shape[0] - 1
     tokens, width = patches.shape[1:]
-    plan, patch, mods, gains, own = stage(
+    plan, patch, mods, gains, own, *half = stage(
         section_bounds, tile_neighbours.T, positions, timesteps, patches[0], modulation, query_gain, own_hbm
     )
     units = tokens // UNIT
@@ -296,7 +363,7 @@
         pieces = [
             from_behind(
                 run_section(
-                    tick, starts[chunk], sizes[chunk], cycle_size, pipe, width, plan, piece, mods, gains, own, other
+                    tick, starts[chunk], sizes[chunk], cycle_size, pipe, width, plan, piece, mods, gains, own, other, half if tick == 0 else []
                 ),
                 "segment",
                 1,

time: 32.4 us -> 33.4 us (1.031); the launches traced: 32.3 us -> 33.7 us
  starting transfers between devices: 12.7 us -> 6.21 us
  Pallas kernels: 8.73 us -> 13.8 us
  waiting for transfers between devices: 9.57 us -> 12.3 us
    ppermute x7, starting transfers between devices: 12.7 us -> 6.21 us  [from_behind(): lax.ppermute(x, axis, [(i, (i + by) % devices) for i in range(devices)])]
    pallas_call x6, Pallas kernels: 5.25 us -> 9.33 us  [run_section(): pl.pallas_call(functools.partial(section_kernel, tick, start, cycle_size,...]
    ppermute x7, waiting for transfers between devices: 9.57 us -> 12.3 us  [from_behind(): lax.ppermute(x, axis, [(i, (i + by) % devices) for i in range(devices)])]
    pallas_call x1, Pallas kernels: 2.11 us -> 3.09 us  [stage(): pl.pallas_call(stage_kernel, out_shape=(pltpu.SMEM((plan_size,), jnp.int3...]
  transfers between devices with their start and end apart: 7 -> 7, of which waited for: 6 -> 6; matrix products, arithmetic and copies ran while one was open for 0% -> 0% of each run, Pallas kernels for 22% -> 35%
where the time goes in v4:
time: 33.4 us; the launch traced here: 33.7 us
  Pallas kernels  13.8 us (41%)
  waiting for transfers between devices  12.3 us (37%)
  starting transfers between devices  6.21 us (19%)
  between operations  1.39 us (4%)
    ppermute x7, waiting for transfers between devices, from_behind(): lax.ppermute(x, axis, [(i, (i + by) % devices) for i in range(devices)])  12.3 us
    pallas_call x6, Pallas kernels, run_section(): pl.pallas_call(functools.partial(section_kernel, tick, start, cycle_size,...  9.33 us
    ppermute x7, starting transfers between devices, from_behind(): lax.ppermute(x, axis, [(i, (i + by) % devices) for i in range(devices)])  6.21 us
    pallas_call x1, Pallas kernels, stage(): pl.pallas_call(stage_kernel, out_shape=(pltpu.SMEM((plan_size,), jnp.int3...  3.09 us
    pallas_call x2, Pallas kernels, place(): pl.pallas_call(functools.partial(place_kernel, starts), out_shape=pltpu.H...  1.37 us
  transfers between devices with their start and end apart: 7, of which 6 were waited for; matrix products, arithmetic and copies ran while one was open for 0% of the time, Pallas kernels for 35%

profile of v4, /device:TPU:0, one launch (start us, length us, event | category | flops | bytes accessed | tf_op | source)
XLA Modules:
  0.0 33.7 jit_solution(16774949254851565439)
XLA Ops:
  0.0 0.5 %collective-permute-start = (bf16[2,2,256,1536]{3,2,1,0:T(8,128)(2,1)}, bf16[2,2,256,1536]{3,2,1,0:T(8,128)(2,1)S(1)}, u32[]{:S(2)}, u32[]{:S(2)}) collective-permute-start(bf16[2,2,256,1536]{3,2,1,0:T(8,128)(2,1)} %bitcast.4), channel_id=1, source_target_pairs={{0,1},{1,0},{2,3},{3,2},{4,5},{5,4},{6,7},{7,6},{8,9},{9,8},{10,11... | collective-permute-start | bytes 9437192 | tf_op jit(solution)/shard_map/ppermute | solution.py:23
  1.8 3.1 %stage.1 = (s32[8]{0:T(128)S(4)}, bf16[128,1536]{1,0:T(8,128)(2,1)S(1)}, bf16[2,3,3,1536]{3,2,1,0:T(4,128)(2,1)S(1)}, f32[12,128]{1,0:T(8,128)S(1)}, bf16[2,2,25...) custom-call(s32[9]{0:T(128)} %bounds_hbm.1, ...), custom_call_target="tpu_custom_call" | custom-call | flops 100000000 | bytes 8000000 | tf_op jit(solution)/shard_map/stage/pallas_call | solution.py:165
  4.9 1.1 %collective-permute-done.other_ref = bf16[2,2,256,1536]{3,2,1,0:T(8,128)(2,1)S(1)} collective-permute-done((bf16[2,2,256,1536]{3,2,1,0:T(8,128)(2,1)}, bf16[2,2,256,1536]{3,2,1,0:T(8,128)(2,1)S(1)}, u32[]{:S(2)}, u32[]{:S(2)}) %collective-permute-start) | collective-permute-done | bytes 3145760 | tf_op jit(solution)/shard_map/ppermute | solution.py:23
  6.0 1.4 %section_0_0.1 = bf16[584,128]{1,0:T(8,128)(2,1)S(1)} custom-call(s32[8]{0:T(128)S(4)} %get-tuple-element.14.plan_ref, bf16[128,1536]{1,0:T(8,128)(2,1)S(1)} %get-tuple-element.15.patch_ref, bf16[2,3,3,1536]{3,2,1,0:T(4,128)(2,1)S(1)} %get-tuple-element.16.modulation_ref, f32[12,128]{1,0:T(8,128)S(1)} %get-tuple-element.17.gain_ref, ...), custom_call_target="tpu_custom_call" | custom-call | flops 400000000 | bytes 8000000 | tf_op jit(solution)/shard_map/section_0_0/pallas_call | solution.py:307
  7.4 2.0 %collective-permute-start.3 = (bf16[584,128]{1,0:T(8,128)(2,1)S(1)}, bf16[584,128]{1,0:T(8,128)(2,1)S(1)}, u32[]{:S(2)}, u32[]{:S(2)}) collective-permute-start(bf16[584,128]{1,0:T(8,128)(2,1)S(1)} %section_0_0.1), channel_id=1, source_target_pairs={{0,2},{2,4},{4,6},{6,8},{8,10},{10,12},{12,14},{14,0},{1,3},{3,5},... | collective-permute-start | bytes 448520 | tf_op jit(solution)/shard_map/ppermute | solution.py:23
  9.4 1.4 %section_0_48.1 = bf16[584,128]{1,0:T(8,128)(2,1)S(1)} custom-call(s32[8]{0:T(128)S(4)} %get-tuple-element.14.plan_ref, bf16[128,1536]{1,0:T(8,128)(2,1)S(1)} %get-tuple-element.15.patch_ref, bf16[2,3,3,1536]{3,2,1,0:T(4,128)(2,1)S(1)} %get-tuple-element.16.modulation_ref, f32[12,128]{1,0:T(8,128)S(1)} %get-tuple-element.17.gain_ref, ...), custom_call_target="tpu_custom_call" | custom-call | flops 400000000 | bytes 8000000 | tf_op jit(solution)/shard_map/section_0_48/pallas_call | solution.py:307
  10.8 1.6 %collective-permute-start.5 = (bf16[584,128]{1,0:T(8,128)(2,1)S(1)}, bf16[584,128]{1,0:T(8,128)(2,1)S(1)}, u32[]{:S(2)}, u32[]{:S(2)}) collective-permute-start(bf16[584,128]{1,0:T(8,128)(2,1)S(1)} %section_0_48.1), channel_id=1, source_target_pairs={{0,2},{2,4},{4,6},{6,8},{8,10},{10,12},{12,14},{14,0},{1,3},{3,5},... | collective-permute-start | bytes 448520 | tf_op jit(solution)/shard_map/ppermute | solution.py:23
  12.4 1.3 %section_0_96.1 = bf16[392,128]{1,0:T(8,128)(2,1)S(1)} custom-call(s32[8]{0:T(128)S(4)} %get-tuple-element.14.plan_ref, bf16[128,1536]{1,0:T(8,128)(2,1)S(1)} %get-tuple-element.15.patch_ref, bf16[2,3,3,1536]{3,2,1,0:T(4,128)(2,1)S(1)} %get-tuple-element.16.modulation_ref, f32[12,128]{1,0:T(8,128)S(1)} %get-tuple-element.17.gain_ref, ...), custom_call_target="tpu_custom_call" | custom-call | flops 400000000 | bytes 8000000 | tf_op jit(solution)/shard_map/section_0_96/pallas_call | solution.py:307
  13.7 1.6 %collective-permute-start.1 = (bf16[392,128]{1,0:T(8,128)(2,1)S(1)}, bf16[392,128]{1,0:T(8,128)(2,1)S(1)}, u32[]{:S(2)}, u32[]{:S(2)}) collective-permute-start(bf16[392,128]{1,0:T(8,128)(2,1)S(1)} %section_0_96.1), channel_id=1, source_target_pairs={{0,2},{2,4},{4,6},{6,8},{8,10},{10,12},{12,14},{14,0},{1,3},{3,5},... | collective-permute-start | bytes 301064 | tf_op jit(solution)/shard_map/ppermute | solution.py:23
  15.4 2.7 %collective-permute-done.3.patch_ref = bf16[584,128]{1,0:T(8,128)(2,1)S(1)} collective-permute-done((bf16[584,128]{1,0:T(8,128)(2,1)S(1)}, bf16[584,128]{1,0:T(8,128)(2,1)S(1)}, u32[]{:S(2)}, u32[]{:S(2)}) %collective-permute-start.3) | collective-permute-done | bytes 149536 | tf_op jit(solution)/shard_map/ppermute | solution.py:23
  18.1 1.8 %section_1_0.1 = bf16[48,1536]{1,0:T(8,128)(2,1)S(1)} custom-call(s32[8]{0:T(128)S(4)} %get-tuple-element.14.plan_ref, bf16[584,128]{1,0:T(8,128)(2,1)S(1)} %collective-permute-done.3.patch_ref, bf16[2,3,3,1536]{3,2,1,0:T(4,128)(2,1)S(1)} %get-tuple-element.16.modulation_ref, f32[12,128]{1,0:T(8,128)S(1)} %get-tuple-element.17.gain_ref, ...), custom_call_target="tpu_custom_call" | custom-call | flops 400000000 | bytes 8000000 | tf_op jit(solution)/shard_map/section_1_0/pallas_call | solution.py:307
  19.9 0.1 collective-permute-start.4
  19.9 1.4 %collective-permute-done.5.patch_ref = bf16[584,128]{1,0:T(8,128)(2,1)S(1)} collective-permute-done((bf16[584,128]{1,0:T(8,128)(2,1)S(1)}, bf16[584,128]{1,0:T(8,128)(2,1)S(1)}, u32[]{:S(2)}, u32[]{:S(2)}) %collective-permute-start.5) | collective-permute-done | bytes 149536 | tf_op jit(solution)/shard_map/ppermute | solution.py:23
  21.3 1.8 %section_1_48.1 = bf16[48,1536]{1,0:T(8,128)(2,1)S(1)} custom-call(s32[8]{0:T(128)S(4)} %get-tuple-element.14.plan_ref, bf16[584,128]{1,0:T(8,128)(2,1)S(1)} %collective-permute-done.5.patch_ref, bf16[2,3,3,1536]{3,2,1,0:T(4,128)(2,1)S(1)} %get-tuple-element.16.modulation_ref, f32[12,128]{1,0:T(8,128)S(1)} %get-tuple-element.17.gain_ref, ...), custom_call_target="tpu_custom_call" | custom-call | flops 400000000 | bytes 8000000 | tf_op jit(solution)/shard_map/section_1_48/pallas_call | solution.py:307
  23.1 0.1 collective-permute-start.6
  23.1 0.0 collective-permute-done.1.patch_ref
  23.1 1.7 %section_1_96.1 = bf16[32,1536]{1,0:T(8,128)(2,1)S(1)} custom-call(s32[8]{0:T(128)S(4)} %get-tuple-element.14.plan_ref, bf16[392,128]{1,0:T(8,128)(2,1)S(1)} %collective-permute-done.1.patch_ref, bf16[2,3,3,1536]{3,2,1,0:T(4,128)(2,1)S(1)} %get-tuple-element.16.modulation_ref, f32[12,128]{1,0:T(8,128)S(1)} %get-tuple-element.17.gain_ref, ...), custom_call_target="tpu_custom_call" | custom-call | flops 400000000 | bytes 8000000 | tf_op jit(solution)/shard_map/section_1_96/pallas_call | solution.py:307
  24.8 0.4 %collective-permute-start.2 = (bf16[32,1536]{1,0:T(8,128)(2,1)S(1)}, bf16[32,1536]{1,0:T(8,128)(2,1)S(1)}, u32[]{:S(2)}, u32[]{:S(2)}) collective-permute-start(bf16[32,1536]{1,0:T(8,128)(2,1)S(1)} %section_1_96.1), channel_id=1, source_target_pairs={{0,2},{2,4},{4,6},{6,8},{8,10},{10,12},{12,14},{14,0},{1,3},{3,5},... | collective-permute-start | bytes 294920 | tf_op jit(solution)/shard_map/ppermute | solution.py:23
  25.2 2.9 %collective-permute-done.4.refs_0_ = bf16[48,1536]{1,0:T(8,128)(2,1)S(1)} collective-permute-done((bf16[48,1536]{1,0:T(8,128)(2,1)S(1)}, bf16[48,1536]{1,0:T(8,128)(2,1)S(1)}, u32[]{:S(2)}, u32[]{:S(2)}) %collective-permute-start.4) | collective-permute-done | bytes 147488 | tf_op jit(solution)/shard_map/ppermute | solution.py:23
  28.1 3.9 %collective-permute-done.6.refs_1_ = bf16[48,1536]{1,0:T(8,128)(2,1)S(1)} collective-permute-done((bf16[48,1536]{1,0:T(8,128)(2,1)S(1)}, bf16[48,1536]{1,0:T(8,128)(2,1)S(1)}, u32[]{:S(2)}, u32[]{:S(2)}) %collective-permute-start.6) | collective-permute-done | bytes 147488 | tf_op jit(solution)/shard_map/ppermute | solution.py:23
  32.0 0.7 %place_0.1.refs_1_ = bf16[128,1536]{1,0:T(8,128)(2,1)} custom-call(bf16[48,1536]{1,0:T(8,128)(2,1)S(1)} %collective-permute-done.4.refs_0_, bf16[48,1536]{1,0:T(8,128)(2,1)S(1)} %collective-permute-done.6.refs_1_), custom_call_target="tpu_custom_call" | custom-call | bytes 600000 | tf_op jit(solution)/shard_map/place_0/pallas_call | solution.py:334
  32.8 0.3 collective-permute-done.2.refs_0_
  33.1 0.6 %place_96.1 = bf16[128,1536]{1,0:T(8,128)(2,1)} custom-call(bf16[32,1536]{1,0:T(8,128)(2,1)S(1)} %collective-permute-done.2.refs_0_, bf16[128,1536]{1,0:T(8,128)(2,1)} %place_0.1.refs_1_), custom_call_target="tpu_custom_call", output_to_operand_aliasing={{}: (1, {})} | custom-call | bytes 600000 | tf_op jit(solution)/shard_map/place_96/pallas_call | solution.py:334
Async XLA Ops:
  0.0 6.0 %collective-permute-start = (bf16[2,2,256,1536]{3,2,1,0:T(8,128)(2,1)}, bf16[2,2,256,1536]{3,2,1,0:T(8,128)(2,1)S(1)}, u32[]{:S(2)}, u32[]{:S(2)}) collective-permute-start(bf16[2,2,256,1536]{3,2,1,0:T(8,128)(2,1)} %bitcast.4), channel_id=1, source_target_pairs={{0,1},{1,0},{2,3},{3,2},{4,5},{5,4},{6,7},{7,6},{8,9},{9,8},{10,11... | collective-permute-start | bytes 9437192 | tf_op jit(solution)/shard_map/ppermute | solution.py:23
  7.4 10.7 %collective-permute-start.3 = (bf16[584,128]{1,0:T(8,128)(2,1)S(1)}, bf16[584,128]{1,0:T(8,128)(2,1)S(1)}, u32[]{:S(2)}, u32[]{:S(2)}) collective-permute-start(bf16[584,128]{1,0:T(8,128)(2,1)S(1)} %section_0_0.1), channel_id=1, source_target_pairs={{0,2},{2,4},{4,6},{6,8},{8,10},{10,12},{12,14},{14,0},{1,3},{3,5},... | collective-permute-start | bytes 448520 | tf_op jit(solution)/shard_map/ppermute | solution.py:23
  10.8 10.5 %collective-permute-start.5 = (bf16[584,128]{1,0:T(8,128)(2,1)S(1)}, bf16[584,128]{1,0:T(8,128)(2,1)S(1)}, u32[]{:S(2)}, u32[]{:S(2)}) collective-permute-start(bf16[584,128]{1,0:T(8,128)(2,1)S(1)} %section_0_48.1), channel_id=1, source_target_pairs={{0,2},{2,4},{4,6},{6,8},{8,10},{10,12},{12,14},{14,0},{1,3},{3,5},... | collective-permute-start | bytes 448520 | tf_op jit(solution)/shard_map/ppermute | solution.py:23
  13.7 9.4 %collective-permute-start.1 = (bf16[392,128]{1,0:T(8,128)(2,1)S(1)}, bf16[392,128]{1,0:T(8,128)(2,1)S(1)}, u32[]{:S(2)}, u32[]{:S(2)}) collective-permute-start(bf16[392,128]{1,0:T(8,128)(2,1)S(1)} %section_0_96.1), channel_id=1, source_target_pairs={{0,2},{2,4},{4,6},{6,8},{8,10},{10,12},{12,14},{14,0},{1,3},{3,5},... | collective-permute-start | bytes 301064 | tf_op jit(solution)/shard_map/ppermute | solution.py:23
  19.9 8.2 %collective-permute-start.4 = (bf16[48,1536]{1,0:T(8,128)(2,1)S(1)}, bf16[48,1536]{1,0:T(8,128)(2,1)S(1)}, u32[]{:S(2)}, u32[]{:S(2)}) collective-permute-start(bf16[48,1536]{1,0:T(8,128)(2,1)S(1)} %section_1_0.1), channel_id=1, source_target_pairs={{0,2},{2,4},{4,6},{6,8},{8,10},{10,12},{12,14},{14,0},{1,3},{3,5},... | collective-permute-start | bytes 442376 | tf_op jit(solution)/shard_map/ppermute | solution.py:23
  23.1 8.9 %collective-permute-start.6 = (bf16[48,1536]{1,0:T(8,128)(2,1)S(1)}, bf16[48,1536]{1,0:T(8,128)(2,1)S(1)}, u32[]{:S(2)}, u32[]{:S(2)}) collective-permute-start(bf16[48,1536]{1,0:T(8,128)(2,1)S(1)} %section_1_48.1), channel_id=1, source_target_pairs={{0,2},{2,4},{4,6},{6,8},{8,10},{10,12},{12,14},{14,0},{1,3},{3,5},... | collective-permute-start | bytes 442376 | tf_op jit(solution)/shard_map/ppermute | solution.py:23
  24.8 8.2 %collective-permute-start.2 = (bf16[32,1536]{1,0:T(8,128)(2,1)S(1)}, bf16[32,1536]{1,0:T(8,128)(2,1)S(1)}, u32[]{:S(2)}, u32[]{:S(2)}) collective-permute-start(bf16[32,1536]{1,0:T(8,128)(2,1)S(1)} %section_1_96.1), channel_id=1, source_target_pairs={{0,2},{2,4},{4,6},{6,8},{8,10},{10,12},{12,14},{14,0},{1,3},{3,5},... | collective-permute-start | bytes 294920 | tf_op jit(solution)/shard_map/ppermute | solution.py:23

commit v5 on v4

--- a/solution.py
+++ b/solution.py
@@ -76,9 +76,7 @@
     gain_out,
     own_out,
     query_out,
-    share_out,
-    top_out,
-    total_out,
+    score_out,
     bounds_ref,
     neighbours_ref,
     sems,
@@ -131,7 +129,6 @@
     head_dim = gain_ref.shape[1]
     blocks = head_blocks(width, head_dim)
     own_row = pl.multiple_of(plan_ref[4 + position_ref[0]] * tile, tile)
-    scale = head_dim ** -0.5 * math.log2(math.e)
     mods = modulation_out[0, step_ref[0]].astype(jnp.float32)
     gain = gain_out[pl.ds(first_layer, 1), :]
     state = [patch_out[:, cols].astype(jnp.float32) for cols in blocks]
@@ -139,22 +136,9 @@
     scores = [
         transposed_dot(query, own_out[0, 0, pl.ds(own_row, tile), cols]) for query, cols in zip(queries, blocks)
     ]
-    tops = [jnp.max(part, axis=-1, keepdims=True) for part in scores]
-    weights = [jnp.exp2((part - top) * scale) for part, top in zip(scores, tops)]
-    totals = [jnp.sum(part, axis=-1, keepdims=True) for part in weights]
-    shares = [
-        jnp.dot(
-            part.astype(jnp.bfloat16),
-            own_out[0, 1, pl.ds(own_row, tile), cols],
-            preferred_element_type=jnp.float32,
-        )
-        for part, cols in zip(weights, blocks)
-    ]
-    for head, cols in enumerate(blocks):
-        query_out[:, cols] = queries[head]
-        share_out[:, cols] = shares[head]
-        top_out[:, cols] = jnp.broadcast_to(tops[head], shares[head].shape)
-        total_out[:, cols] = jnp.broadcast_to(totals[head], shares[head].shape)
+    for query, part, cols in zip(queries, scores, blocks):
+        query_out[:, cols] = query
+        score_out[:, cols] = part
     for copy in slabs[1:]:
         copy.wait()
 
@@ -172,11 +156,9 @@
             pltpu.VMEM(own.shape, own.dtype),
             pltpu.VMEM(patch.shape, jnp.bfloat16),
             pltpu.VMEM(patch.shape, jnp.float32),
-            pltpu.VMEM(patch.shape, jnp.float32),
-            pltpu.VMEM(patch.shape, jnp.float32),
         ),
         in_specs=[ANY] * 2 + [SMEM] * 2 + [ANY] * 4,
-        out_specs=(SMEM,) + (VMEM,) * 8,
+        out_specs=(SMEM,) + (VMEM,) * 6,
         scratch_shapes=[pltpu.SMEM(x.shape, x.dtype) for x in (bounds, neighbours)]
         + [pltpu.SemaphoreType.DMA((4 + 2 * slots,))],
         compiler_params=pltpu.CompilerParams(vmem_limit_bytes=16 << 20),
@@ -246,27 +228,28 @@
 
         def tiles(kind, cols):
             theirs = other_ref[slot, kind, pl.ds(other_row, tile), cols]
-            if split:
+            if split and kind == 0:
                 return theirs
             return jnp.concatenate([own_ref[slot, kind, pl.ds(own_row, tile), cols], theirs])
 
         state = [state_ref[:, cols] for cols in blocks]
         if split:
-            query_ref, share_ref, top_ref, total_ref = half
+            query_ref, score_ref = half
             window = slice(start, start + rows)
             queries = [query_ref[window, cols] for cols in blocks]
         else:
             queries = modulated_queries(state, mods, gain, blocks, width)
         paired = paired_queries(queries)
         scores = [transposed_dot(query, tiles(0, cols)) for query, cols in zip(paired, doubles)]
+        if split:
+            scores = [
+                jnp.concatenate(
+                    [jnp.concatenate([score_ref[window, blocks[head]], score_ref[window, blocks[head + 1]]]), part],
+                    axis=1,
+                )
+                for head, part in zip(pairs, scores)
+            ]
         tops = [jnp.max(part, axis=-1, keepdims=True) for part in scores]
-        if split:
-            own_tops = [
-                jnp.concatenate([top_ref[window, blocks[head]], top_ref[window, blocks[head + 1]]])
-                for head in pairs
-            ]
-            tops = [jnp.maximum(top, own_top) for top, own_top in zip(tops, own_tops)]
-            fades = [jnp.exp2((own_top - top) * scale) for top, own_top in zip(tops, own_tops)]
         weights = [jnp.exp2((part - top) * scale) for part, top in zip(scores, tops)]
         totals = [jnp.sum(part, axis=-1, keepdims=True) for part in weights]
         blended = [
@@ -278,13 +261,8 @@
                 head = 2 * pair + side
                 cols = blocks[head]
                 span = slice(side * rows, (side + 1) * rows)
-                share = blend[span, side * head_dim : (side + 1) * head_dim]
-                whole = total[span]
-                if split:
-                    fade = fades[pair][span]
-                    share = share + fade * share_ref[window, cols]
-                    whole = whole + fade * total_ref[window, cols]
-                state_ref[:, cols] = state[head] + mods[2:3, cols] * (share / whole)
+                share = blend[span, side * head_dim : (side + 1) * head_dim] / total[span]
+                state_ref[:, cols] = state[head] + mods[2:3, cols] * share
 
     layer(0)
     for slot in range(1, slots):

time: 33.4 us -> 33.4 us (level); the launches traced: 33.7 us -> 32.8 us
  starting transfers between devices: 6.21 us -> 12.2 us
  Pallas kernels: 13.8 us -> 8.3 us
  waiting for transfers between devices: 12.3 us -> 11 us
    ppermute x7, starting transfers between devices: 6.21 us -> 12.2 us  [from_behind(): lax.ppermute(x, axis, [(i, (i + by) % devices) for i in range(devices)])]
    pallas_call x6, Pallas kernels: 9.33 us -> 4.17 us  [run_section(): pl.pallas_call(functools.partial(section_kernel, tick, start, cycle_size,...]
    ppermute x7, waiting for transfers between devices: 12.3 us -> 11 us  [from_behind(): lax.ppermute(x, axis, [(i, (i + by) % devices) for i in range(devices)])]
    pallas_call x1, Pallas kernels: 3.09 us -> 2.76 us  [stage(): pl.pallas_call(stage_kernel, out_shape=(pltpu.SMEM((plan_size,), jnp.int3...]
  transfers between devices with their start and end apart: 7 -> 7, of which waited for: 6 -> 6; matrix products, arithmetic and copies ran while one was open for 0% -> 0% of each run, Pallas kernels for 35% -> 22%
where the time goes in v5:
time: 33.4 us; the launch traced here: 32.8 us
  starting transfers between devices  12.2 us (37%)
  waiting for transfers between devices  11 us (33%)
  Pallas kernels  8.3 us (25%)
  between operations  1.37 us (4%)
    ppermute x7, starting transfers between devices, from_behind(): lax.ppermute(x, axis, [(i, (i + by) % devices) for i in range(devices)])  12.2 us
    ppermute x7, waiting for transfers between devices, from_behind(): lax.ppermute(x, axis, [(i, (i + by) % devices) for i in range(devices)])  11 us
    pallas_call x6, Pallas kernels, run_section(): pl.pallas_call(functools.partial(section_kernel, tick, start, cycle_size,...  4.17 us
    pallas_call x1, Pallas kernels, stage(): pl.pallas_call(stage_kernel, out_shape=(pltpu.SMEM((plan_size,), jnp.int3...  2.76 us
    pallas_call x2, Pallas kernels, place(): pl.pallas_call(functools.partial(place_kernel, starts), out_shape=pltpu.H...  1.37 us
  transfers between devices with their start and end apart: 7, of which 6 were waited for; matrix products, arithmetic and copies ran while one was open for 0% of the time, Pallas kernels for 22%

profile of v5, /device:TPU:0, one launch (start us, length us, event | category | flops | bytes accessed | tf_op | source)
XLA Modules:
  0.0 32.8 jit_solution(10112297190162114029)
XLA Ops:
  0.0 0.5 %collective-permute-start = (bf16[2,2,256,1536]{3,2,1,0:T(8,128)(2,1)}, bf16[2,2,256,1536]{3,2,1,0:T(8,128)(2,1)S(1)}, u32[]{:S(2)}, u32[]{:S(2)}) collective-permute-start(bf16[2,2,256,1536]{3,2,1,0:T(8,128)(2,1)} %bitcast.4), channel_id=1, source_target_pairs={{0,1},{1,0},{2,3},{3,2},{4,5},{5,4},{6,7},{7,6},{8,9},{9,8},{10,11... | collective-permute-start | bytes 9437192 | tf_op jit(solution)/shard_map/ppermute | solution.py:23
  1.8 2.8 %stage.1 = (s32[8]{0:T(128)S(4)}, bf16[128,1536]{1,0:T(8,128)(2,1)S(1)}, bf16[2,3,3,1536]{3,2,1,0:T(4,128)(2,1)S(1)}, f32[12,128]{1,0:T(8,128)S(1)}, bf16[2,2,25...) custom-call(s32[9]{0:T(128)} %bounds_hbm.1, s32[2,4]{1,0:T(2,128)} %bitcast.7, ...), custom_call_target="tpu_custom_call" | custom-call | flops 100000000 | bytes 8000000 | tf_op jit(solution)/shard_map/stage/pallas_call | solution.py:149
  4.6 1.4 %collective-permute-done.other_ref = bf16[2,2,256,1536]{3,2,1,0:T(8,128)(2,1)S(1)} collective-permute-done((bf16[2,2,256,1536]{3,2,1,0:T(8,128)(2,1)}, bf16[2,2,256,1536]{3,2,1,0:T(8,128)(2,1)S(1)}, u32[]{:S(2)}, u32[]{:S(2)}) %collective-permute-start) | collective-permute-done | bytes 3145760 | tf_op jit(solution)/shard_map/ppermute | solution.py:23
  6.0 0.5 %section_0_0.1 = bf16[584,128]{1,0:T(8,128)(2,1)S(1)} custom-call(s32[8]{0:T(128)S(4)} %get-tuple-element.12.plan_ref, bf16[128,1536]{1,0:T(8,128)(2,1)S(1)} %get-tuple-element.13.patch_ref, bf16[2,3,3,1536]{3,2,1,0:T(4,128)(2,1)S(1)} %get-tuple-element.14.modulation_ref, f32[12,128]{1,0:T(8,128)S(1)} %get-tuple-element.15.gain_ref, ...), custom_call_target="tpu_custom_call" | custom-call | flops 400000000 | bytes 8000000 | tf_op jit(solution)/shard_map/section_0_0/pallas_call | solution.py:285
  6.5 3.8 %collective-permute-start.3 = (bf16[584,128]{1,0:T(8,128)(2,1)S(1)}, bf16[584,128]{1,0:T(8,128)(2,1)S(1)}, u32[]{:S(2)}, u32[]{:S(2)}) collective-permute-start(bf16[584,128]{1,0:T(8,128)(2,1)S(1)} %section_0_0.1), channel_id=1, source_target_pairs={{0,2},{2,4},{4,6},{6,8},{8,10},{10,12},{12,14},{14,0},{1,3},{3,5},... | collective-permute-start | bytes 448520 | tf_op jit(solution)/shard_map/ppermute | solution.py:23
  10.3 0.5 %section_0_48.1 = bf16[584,128]{1,0:T(8,128)(2,1)S(1)} custom-call(s32[8]{0:T(128)S(4)} %get-tuple-element.12.plan_ref, bf16[128,1536]{1,0:T(8,128)(2,1)S(1)} %get-tuple-element.13.patch_ref, bf16[2,3,3,1536]{3,2,1,0:T(4,128)(2,1)S(1)} %get-tuple-element.14.modulation_ref, f32[12,128]{1,0:T(8,128)S(1)} %get-tuple-element.15.gain_ref, ...), custom_call_target="tpu_custom_call" | custom-call | flops 400000000 | bytes 8000000 | tf_op jit(solution)/shard_map/section_0_48/pallas_call | solution.py:285
  10.8 2.5 %collective-permute-start.5 = (bf16[584,128]{1,0:T(8,128)(2,1)S(1)}, bf16[584,128]{1,0:T(8,128)(2,1)S(1)}, u32[]{:S(2)}, u32[]{:S(2)}) collective-permute-start(bf16[584,128]{1,0:T(8,128)(2,1)S(1)} %section_0_48.1), channel_id=1, source_target_pairs={{0,2},{2,4},{4,6},{6,8},{8,10},{10,12},{12,14},{14,0},{1,3},{3,5},... | collective-permute-start | bytes 448520 | tf_op jit(solution)/shard_map/ppermute | solution.py:23
  13.3 0.5 %section_0_96.1 = bf16[392,128]{1,0:T(8,128)(2,1)S(1)} custom-call(s32[8]{0:T(128)S(4)} %get-tuple-element.12.plan_ref, bf16[128,1536]{1,0:T(8,128)(2,1)S(1)} %get-tuple-element.13.patch_ref, bf16[2,3,3,1536]{3,2,1,0:T(4,128)(2,1)S(1)} %get-tuple-element.14.modulation_ref, f32[12,128]{1,0:T(8,128)S(1)} %get-tuple-element.15.gain_ref, ...), custom_call_target="tpu_custom_call" | custom-call | flops 400000000 | bytes 8000000 | tf_op jit(solution)/shard_map/section_0_96/pallas_call | solution.py:285
  13.8 2.4 %collective-permute-start.1 = (bf16[392,128]{1,0:T(8,128)(2,1)S(1)}, bf16[392,128]{1,0:T(8,128)(2,1)S(1)}, u32[]{:S(2)}, u32[]{:S(2)}) collective-permute-start(bf16[392,128]{1,0:T(8,128)(2,1)S(1)} %section_0_96.1), channel_id=1, source_target_pairs={{0,2},{2,4},{4,6},{6,8},{8,10},{10,12},{12,14},{14,0},{1,3},{3,5},... | collective-permute-start | bytes 301064 | tf_op jit(solution)/shard_map/ppermute | solution.py:23
  16.2 1.9 %collective-permute-done.3.patch_ref = bf16[584,128]{1,0:T(8,128)(2,1)S(1)} collective-permute-done((bf16[584,128]{1,0:T(8,128)(2,1)S(1)}, bf16[584,128]{1,0:T(8,128)(2,1)S(1)}, u32[]{:S(2)}, u32[]{:S(2)}) %collective-permute-start.3) | collective-permute-done | bytes 149536 | tf_op jit(solution)/shard_map/ppermute | solution.py:23
  18.1 0.9 %section_1_0.1 = bf16[48,1536]{1,0:T(8,128)(2,1)S(1)} custom-call(s32[8]{0:T(128)S(4)} %get-tuple-element.12.plan_ref, bf16[584,128]{1,0:T(8,128)(2,1)S(1)} %collective-permute-done.3.patch_ref, bf16[2,3,3,1536]{3,2,1,0:T(4,128)(2,1)S(1)} %get-tuple-element.14.modulation_ref, f32[12,128]{1,0:T(8,128)S(1)} %get-tuple-element.15.gain_ref, ...), custom_call_target="tpu_custom_call" | custom-call | flops 400000000 | bytes 8000000 | tf_op jit(solution)/shard_map/section_1_0/pallas_call | solution.py:285
  19.0 0.1 collective-permute-start.4
  19.0 2.2 %collective-permute-done.5.patch_ref = bf16[584,128]{1,0:T(8,128)(2,1)S(1)} collective-permute-done((bf16[584,128]{1,0:T(8,128)(2,1)S(1)}, bf16[584,128]{1,0:T(8,128)(2,1)S(1)}, u32[]{:S(2)}, u32[]{:S(2)}) %collective-permute-start.5) | collective-permute-done | bytes 149536 | tf_op jit(solution)/shard_map/ppermute | solution.py:23
  21.3 0.9 %section_1_48.1 = bf16[48,1536]{1,0:T(8,128)(2,1)S(1)} custom-call(s32[8]{0:T(128)S(4)} %get-tuple-element.12.plan_ref, bf16[584,128]{1,0:T(8,128)(2,1)S(1)} %collective-permute-done.5.patch_ref, bf16[2,3,3,1536]{3,2,1,0:T(4,128)(2,1)S(1)} %get-tuple-element.14.modulation_ref, f32[12,128]{1,0:T(8,128)S(1)} %get-tuple-element.15.gain_ref, ...), custom_call_target="tpu_custom_call" | custom-call | flops 400000000 | bytes 8000000 | tf_op jit(solution)/shard_map/section_1_48/pallas_call | solution.py:285
  22.2 0.7 %collective-permute-start.6 = (bf16[48,1536]{1,0:T(8,128)(2,1)S(1)}, bf16[48,1536]{1,0:T(8,128)(2,1)S(1)}, u32[]{:S(2)}, u32[]{:S(2)}) collective-permute-start(bf16[48,1536]{1,0:T(8,128)(2,1)S(1)} %section_1_48.1), channel_id=1, source_target_pairs={{0,2},{2,4},{4,6},{6,8},{8,10},{10,12},{12,14},{14,0},{1,3},{3,5},... | collective-permute-start | bytes 442376 | tf_op jit(solution)/shard_map/ppermute | solution.py:23
  22.9 0.0 collective-permute-done.1.patch_ref
  22.9 0.8 %section_1_96.1 = bf16[32,1536]{1,0:T(8,128)(2,1)S(1)} custom-call(s32[8]{0:T(128)S(4)} %get-tuple-element.12.plan_ref, bf16[392,128]{1,0:T(8,128)(2,1)S(1)} %collective-permute-done.1.patch_ref, bf16[2,3,3,1536]{3,2,1,0:T(4,128)(2,1)S(1)} %get-tuple-element.14.modulation_ref, f32[12,128]{1,0:T(8,128)S(1)} %get-tuple-element.15.gain_ref, ...), custom_call_target="tpu_custom_call" | custom-call | flops 400000000 | bytes 8000000 | tf_op jit(solution)/shard_map/section_1_96/pallas_call | solution.py:285
  23.7 2.3 %collective-permute-start.2 = (bf16[32,1536]{1,0:T(8,128)(2,1)S(1)}, bf16[32,1536]{1,0:T(8,128)(2,1)S(1)}, u32[]{:S(2)}, u32[]{:S(2)}) collective-permute-start(bf16[32,1536]{1,0:T(8,128)(2,1)S(1)} %section_1_96.1), channel_id=1, source_target_pairs={{0,2},{2,4},{4,6},{6,8},{8,10},{10,12},{12,14},{14,0},{1,3},{3,5},... | collective-permute-start | bytes 294920 | tf_op jit(solution)/shard_map/ppermute | solution.py:23
  26.0 1.2 %collective-permute-done.4.refs_0_ = bf16[48,1536]{1,0:T(8,128)(2,1)S(1)} collective-permute-done((bf16[48,1536]{1,0:T(8,128)(2,1)S(1)}, bf16[48,1536]{1,0:T(8,128)(2,1)S(1)}, u32[]{:S(2)}, u32[]{:S(2)}) %collective-permute-start.4) | collective-permute-done | bytes 147488 | tf_op jit(solution)/shard_map/ppermute | solution.py:23
  27.2 3.9 %collective-permute-done.6.refs_1_ = bf16[48,1536]{1,0:T(8,128)(2,1)S(1)} collective-permute-done((bf16[48,1536]{1,0:T(8,128)(2,1)S(1)}, bf16[48,1536]{1,0:T(8,128)(2,1)S(1)}, u32[]{:S(2)}, u32[]{:S(2)}) %collective-permute-start.6) | collective-permute-done | bytes 147488 | tf_op jit(solution)/shard_map/ppermute | solution.py:23
  31.1 0.7 %place_0.1.refs_1_ = bf16[128,1536]{1,0:T(8,128)(2,1)} custom-call(bf16[48,1536]{1,0:T(8,128)(2,1)S(1)} %collective-permute-done.4.refs_0_, bf16[48,1536]{1,0:T(8,128)(2,1)S(1)} %collective-permute-done.6.refs_1_), custom_call_target="tpu_custom_call" | custom-call | bytes 600000 | tf_op jit(solution)/shard_map/place_0/pallas_call | solution.py:312
  31.9 0.3 collective-permute-done.2.refs_0_
  32.2 0.6 %place_96.1 = bf16[128,1536]{1,0:T(8,128)(2,1)} custom-call(bf16[32,1536]{1,0:T(8,128)(2,1)S(1)} %collective-permute-done.2.refs_0_, bf16[128,1536]{1,0:T(8,128)(2,1)} %place_0.1.refs_1_), custom_call_target="tpu_custom_call", output_to_operand_aliasing={{}: (1, {})} | custom-call | bytes 600000 | tf_op jit(solution)/shard_map/place_96/pallas_call | solution.py:312
Async XLA Ops:
  0.0 6.0 %collective-permute-start = (bf16[2,2,256,1536]{3,2,1,0:T(8,128)(2,1)}, bf16[2,2,256,1536]{3,2,1,0:T(8,128)(2,1)S(1)}, u32[]{:S(2)}, u32[]{:S(2)}) collective-permute-start(bf16[2,2,256,1536]{3,2,1,0:T(8,128)(2,1)} %bitcast.4), channel_id=1, source_target_pairs={{0,1},{1,0},{2,3},{3,2},{4,5},{5,4},{6,7},{7,6},{8,9},{9,8},{10,11... | collective-permute-start | bytes 9437192 | tf_op jit(solution)/shard_map/ppermute | solution.py:23
  6.5 11.6 %collective-permute-start.3 = (bf16[584,128]{1,0:T(8,128)(2,1)S(1)}, bf16[584,128]{1,0:T(8,128)(2,1)S(1)}, u32[]{:S(2)}, u32[]{:S(2)}) collective-permute-start(bf16[584,128]{1,0:T(8,128)(2,1)S(1)} %section_0_0.1), channel_id=1, source_target_pairs={{0,2},{2,4},{4,6},{6,8},{8,10},{10,12},{12,14},{14,0},{1,3},{3,5},... | collective-permute-start | bytes 448520 | tf_op jit(solution)/shard_map/ppermute | solution.py:23
  10.8 10.5 %collective-permute-start.5 = (bf16[584,128]{1,0:T(8,128)(2,1)S(1)}, bf16[584,128]{1,0:T(8,128)(2,1)S(1)}, u32[]{:S(2)}, u32[]{:S(2)}) collective-permute-start(bf16[584,128]{1,0:T(8,128)(2,1)S(1)} %section_0_48.1), channel_id=1, source_target_pairs={{0,2},{2,4},{4,6},{6,8},{8,10},{10,12},{12,14},{14,0},{1,3},{3,5},... | collective-permute-start | bytes 448520 | tf_op jit(solution)/shard_map/ppermute | solution.py:23
  13.8 9.1 %collective-permute-start.1 = (bf16[392,128]{1,0:T(8,128)(2,1)S(1)}, bf16[392,128]{1,0:T(8,128)(2,1)S(1)}, u32[]{:S(2)}, u32[]{:S(2)}) collective-permute-start(bf16[392,128]{1,0:T(8,128)(2,1)S(1)} %section_0_96.1), channel_id=1, source_target_pairs={{0,2},{2,4},{4,6},{6,8},{8,10},{10,12},{12,14},{14,0},{1,3},{3,5},... | collective-permute-start | bytes 301064 | tf_op jit(solution)/shard_map/ppermute | solution.py:23
  19.0 8.2 %collective-permute-start.4 = (bf16[48,1536]{1,0:T(8,128)(2,1)S(1)}, bf16[48,1536]{1,0:T(8,128)(2,1)S(1)}, u32[]{:S(2)}, u32[]{:S(2)}) collective-permute-start(bf16[48,1536]{1,0:T(8,128)(2,1)S(1)} %section_1_0.1), channel_id=1, source_target_pairs={{0,2},{2,4},{4,6},{6,8},{8,10},{10,12},{12,14},{14,0},{1,3},{3,5},... | collective-permute-start | bytes 442376 | tf_op jit(solution)/shard_map/ppermute | solution.py:23
  22.2 8.9 %collective-permute-start.6 = (bf16[48,1536]{1,0:T(8,128)(2,1)S(1)}, bf16[48,1536]{1,0:T(8,128)(2,1)S(1)}, u32[]{:S(2)}, u32[]{:S(2)}) collective-permute-start(bf16[48,1536]{1,0:T(8,128)(2,1)S(1)} %section_1_48.1), channel_id=1, source_target_pairs={{0,2},{2,4},{4,6},{6,8},{8,10},{10,12},{12,14},{14,0},{1,3},{3,5},... | collective-permute-start | bytes 442376 | tf_op jit(solution)/shard_map/ppermute | solution.py:23
  23.7 8.4 %collective-permute-start.2 = (bf16[32,1536]{1,0:T(8,128)(2,1)S(1)}, bf16[32,1536]{1,0:T(8,128)(2,1)S(1)}, u32[]{:S(2)}, u32[]{:S(2)}) collective-permute-start(bf16[32,1536]{1,0:T(8,128)(2,1)S(1)} %section_1_96.1), channel_id=1, source_target_pairs={{0,2},{2,4},{4,6},{6,8},{8,10},{10,12},{12,14},{14,0},{1,3},{3,5},... | collective-permute-start | bytes 294920 | tf_op jit(solution)/shard_map/ppermute | solution.py:23
